TPU v7x, 32 devices: a whole 2x2x4 slice. The times are simulated.
32 devices in a mesh: grp: 2 (over x), tpl: 16 (over z, y, core).
Axes of the slice: x: 2, y: 2, z: 4, core: 2. Of those that a mesh axis runs over, the one named last changes fastest.
Arguments:
- strain_slots: bfloat16 [32, 3, 2, 262144], P(('grp', 'tpl')), parts along dimension 0, may hold values from -6 to 6
- templates: bfloat16 [32, 2, 262144], P(None, None, 'tpl'), may hold values from -6 to 6
- cutoffs: int32 [32], replicated, may hold values from 32768 to 262144
- lists: int32 [16, 2], replicated, may hold values from 0 to 31, as said below
- owner: int32 [2], P('grp'), parts along dimension 0, may hold values from 0 to 15
- slides: int32 [6], P('grp'), parts along dimension 0, may hold values from 0 to 262143
Outputs:
- peaks: float32 [64], P(('grp', 'tpl')), parts along dimension 0
- norms: float32 [64], P(('grp', 'tpl')), parts along dimension 0
There are 2 independent parts, one for each index of `grp`. A program takes and returns all parts, laid end to end along the dimension named above; an argument that names none is the same for every part. Nothing has to cross between parts.
Inputs may be any that keep to these rules, and one draw needn't show every extreme that they name: Every template appears once in lists; list positions in row-major order run through the templates by falling cutoffs. One template has cutoff 262144, one has 32768.
All inputs are finite; a program needn't handle non-finite values.
Results may differ from a plain program's by a relative error of at most 0.0021.
Values may be sent and summed in bfloat16 or wider, within the bound.
A program may use at most 128 MiB of HBM per device.

v0:
```python
import jax
import jax.numpy as jnp
from jax import lax
from jax.sharding import PartitionSpec as P

DET = 3
ROWS = 512
COLS = 512
BLOCK_ROWS = 64


two_pi = 6.283185307179586
eps_norm = 1e-06


def spread(block, axis, owner):
    block = jnp.where(lax.axis_index(axis) == owner, block, jnp.zeros_like(block))
    return lax.psum(block, axis)


def turn_table(left_ids, right_ids, period):
    product_idx = left_ids[:, None] * right_ids[None, :] % period
    angles = product_idx.astype(jnp.float32) * (two_pi / period)
    return (jnp.cos(angles), jnp.sin(angles))


def slide_phases(slides):
    total = ROWS * COLS
    bin_ids = jnp.arange(total, dtype=jnp.int32)
    row_ids = bin_ids // COLS
    col_ids = bin_ids % COLS
    stride = COLS * slides % total
    turns = (
        row_ids[None, :] * stride[:, None] % total + col_ids[None, :] * slides[:, None] % total
    ) % total
    angles = turns.astype(jnp.float32) * (two_pi / total)
    return (jnp.cos(angles), jnp.sin(angles))


def body(strain_slots, templates, cutoffs, lists, owner, slides):
    total = ROWS * COLS
    block_count_all = ROWS // BLOCK_ROWS
    devices = lax.axis_size("tpl")
    own_index = lax.axis_index("tpl")
    per_device = lists.shape[1]
    strain = spread(strain_slots[0], "tpl", owner[0])
    flat_list = lists.reshape(-1)
    device_ids = jnp.arange(devices, dtype=jnp.int32)[:, None]
    slot_ids = jnp.arange(per_device, dtype=jnp.int32)[None, :]
    positions = device_ids * per_device + slot_ids
    chosen = flat_list[positions]
    picked = templates[chosen.reshape(-1)]
    picked = picked.reshape(devices, per_device, 2, templates.shape[2])
    arrived = lax.all_to_all(picked, "tpl", split_axis=0, concat_axis=3, tiled=True)[0]
    own_ids = lax.dynamic_index_in_dim(chosen, own_index, 0, keepdims=False)
    cutoff_bins = cutoffs[own_ids]
    row_ids = jnp.arange(ROWS, dtype=jnp.int32)
    col_ids = jnp.arange(COLS, dtype=jnp.int32)
    row_cos, row_sin = turn_table(row_ids, row_ids, ROWS)
    cos_blocks = row_cos.reshape(ROWS, block_count_all, BLOCK_ROWS).transpose(1, 0, 2)
    sin_blocks = row_sin.reshape(ROWS, block_count_all, BLOCK_ROWS).transpose(1, 0, 2)
    row_blocks = jnp.concatenate(
        [
            jnp.concatenate([cos_blocks, -sin_blocks], 2),
            jnp.concatenate([sin_blocks, cos_blocks], 2),
        ],
        1,
    ).astype(jnp.bfloat16)
    twiddle_cos, twiddle_sin = turn_table(row_ids, col_ids, total)
    col_cos, col_sin = turn_table(col_ids, col_ids, COLS)
    col_table = jnp.concatenate(
        [jnp.concatenate([col_cos, col_sin], 1), jnp.concatenate([-col_sin, col_cos], 1)], 0
    ).astype(jnp.bfloat16)
    phase_cos, phase_sin = slide_phases(slides)
    data_re = strain[:, 0].astype(jnp.float32)
    data_im = strain[:, 1].astype(jnp.float32)

    def filter_one(packed):
        waveform, cutoff = packed
        inside = jnp.arange(total, dtype=jnp.int32) < cutoff
        wave_re = waveform[0].astype(jnp.float32)
        wave_im = waveform[1].astype(jnp.float32)
        real_part = data_re * wave_re + data_im * wave_im
        imag_part = data_im * wave_re - data_re * wave_im
        prod_re = jnp.where(inside, real_part * phase_cos - imag_part * phase_sin, 0.0)
        prod_im = jnp.where(inside, real_part * phase_sin + imag_part * phase_cos, 0.0)
        stacked = jnp.concatenate(
            [
                prod_re.reshape(DET, block_count_all, BLOCK_ROWS, COLS),
                prod_im.reshape(DET, block_count_all, BLOCK_ROWS, COLS),
            ],
            2,
        ).astype(jnp.bfloat16)
        section_one = jnp.einsum(
            "bai,dbic->dac", row_blocks, stacked, preferred_element_type=jnp.float32
        )
        first_re = section_one[:, :ROWS]
        first_im = section_one[:, ROWS:]
        twisted = jnp.concatenate(
            [
                first_re * twiddle_cos - first_im * twiddle_sin,
                first_re * twiddle_sin + first_im * twiddle_cos,
            ],
            2,
        ).astype(jnp.bfloat16)
        series = jnp.einsum("dab,bc->dac", twisted, col_table, preferred_element_type=jnp.float32)
        squares = jnp.sum(series * series, axis=0)
        power_sum = squares[:, :COLS] + squares[:, COLS:]
        sigmasq = jnp.sum(jnp.where(inside, wave_re * wave_re + wave_im * wave_im, 0.0))
        return (jnp.max(power_sum) / (2.0 * (sigmasq + eps_norm)), sigmasq / total)

    peaks, norms = lax.map(filter_one, (arrived, cutoff_bins))
    return (peaks, norms)


def solution(mesh):
    in_specs = (
        P(("grp", "tpl"), None, None, None),
        P(None, None, "tpl"),
        P(),
        P(),
        P("grp"),
        P("grp"),
    )
    out_specs = (P(("grp", "tpl")), P(("grp", "tpl")))
    return jax.shard_map(body, mesh=mesh, in_specs=in_specs, out_specs=out_specs, check_vma=False)
```

profile of v0, /device:TPU:0, one launch (start us, length us, event | category | flops | bytes accessed | tf_op | source)
XLA Modules:
  0.0 458.4 jit_solution(1903081071991389454)
XLA Ops:
  8.0 10.3 %fusion.41 = bf16[3,2,262144]{2,0,1:T(4,128)(2,1)} fusion(bf16[1,3,2,262144]{3,2,1,0:T(2,128)(2,1)} %param.8, pred[]{:T(512)S(6)} %eq.15), kind=kLoop, calls=%fused_computation.69 | loop fusion | flops 1572864 | bytes 6291457 | tf_op jit(solution)/shard_map/jit(_where)/select_n | solution.py:17
  19.9 6.1 %gather_fusion.2 = bf16[32,2,16384]{2,1,0:T(2,128)(2,1)} fusion(bf16[32,2,16384]{2,1,0:T(2,128)(2,1)S(1)} %copy-done, s32[1024]{0:T(1024)S(1)} %pad_clamp_fusion), kind=kCustom, calls=%fused_computation.2 | custom fusion | bytes 4194432 | tf_op jit(solution)/shard_map/gather | solution.py:52
  26.0 7.8 %all-to-all-start = ((bf16[16,2,2,16384]{3,2,1,0:T(2,128)(2,1)}), bf16[16,2,2,16384]{3,2,1,0:T(2,128)(2,1)}, u32[]{:S(2)}, u32[]{:S(2)}) async-start(bf16[16,2,2,16384]{3,2,1,0:T(2,128)(2,1)} %bitcast.96), calls=%async_computation | async-start | bytes 4194304 | tf_op jit(solution)/shard_map/all_to_all | solution.py:54
  33.8 1.5 fusion.49
  36.1 4.0 fusion.66
  40.1 4.3 negate_convert_fusion.1
  44.4 8.7 %negate_convert_fusion = (bf16[8,512,64]{2,1,0:T(8,128)(2,1)S(1)}, bf16[8,512,64]{2,1,0:T(8,128)(2,1)S(1)}, bf16[8,512,64]{2,1,0:T(8,128)(2,1)S(1)}) fusion(s32[8,64]{1,0:T(8,128)S(1)} %multiply_add_fusion.2), kind=kLoop, calls=%fused_computation.82 | loop fusion | flops 4718592 | bytes 1574912 | tf_op jit(solution)/shard_map/convert.19
  53.1 2.5 maximum_maximum_fusion
  55.6 1.6 maximum_maximum_fusion.1
  57.2 115.2 %all-reduce.2.cloned.1.call-done = bf16[3,2,262144]{2,0,1:T(4,128)(2,1)} async-done(((bf16[3,2,262144]{2,0,1:T(4,128)(2,1)}), bf16[3,2,262144]{2,0,1:T(4,128)(2,1)}) %all-reduce.2.cloned.1.call-update) | async-done | bytes 3145744 | tf_op jit(solution)/shard_map/psum | solution.py:18
  172.4 5.0 %fusion.45 = (f32[3,262144]{1,0:T(4,128)}, f32[3,262144]{1,0:T(4,128)}) fusion(bf16[3,2,262144]{2,0,1:T(4,128)(2,1)} %all-reduce.2.cloned.1.call-done), kind=kLoop, calls=%fused_computation.77 | loop fusion | flops 1572864 | bytes 9437184 | tf_op jit(solution)/shard_map/convert_element_type | solution.py:76
  177.4 2.7 copy.68
  180.1 2.5 squeeze.23
  182.7 267.2 %while.15 = (s32[]{:T(128)}, f32[2]{0:T(128)S(1)}, f32[2]{0:T(128)S(1)}, s32[2]{0:T(128)S(1)}, f32[3,262144]{1,0:T(4,128)}, /*index=5*/bf16[2,2,262144]{2,1,0:T(...) while((s32[]{:T(128)}, f32[2]{0:T(128)S(1)}, ...), condition=%wide.region_5.6_spmd.clone.clone.clone, body=%wide.region_1.5_spmd.clone.clone.clone.sunk | while | flops 6514016256 | bytes 146276784 | solution.py:112
  183.0 16.5 %fusion.84 = (f32[262144]{0:T(1024)}, f32[262144]{0:T(1024)S(1)}, f32[1,1,262144]{2,1,0:T(1,128)}) fusion(bf16[2,2,262144]{2,1,0:T(2,128)(2,1)} %get-tuple-element.387, s32[]{:T(128)} %get-tuple-element.363, s32[]{:T(128)S(6)} %add.959), kind=kLoop, calls=%fused_computation.62.clone.1 | loop fusion | flops 1310720 | bytes 4194312 | tf_op jit(solution)/shard_map/while/body/eval_jaxpr/convert_element_type | solution.py:81
  200.3 1.4 reshape.324
  201.7 1.9 copy.97
  205.2 42.2 %fusion.83 = (f32[3,262144]{1,0:T(4,128)S(1)}, f32[3,262144]{1,0:T(4,128)}) fusion(s32[3]{0:T(128)S(1)} %get-tuple-element.393, s32[262144]{0:T(1024)} %get-tuple-element.394, s32[3]{0:T(128)S(1)} %get-tuple-element.391, s32[262144]{0:T(1024)} %get-tuple-element.392), kind=kLoop, calls=%fused_computation.43.clone.1 | loop fusion | flops 29884416 | bytes 8388632 | tf_op jit(solution)/shard_map/sin | solution.py:37
  247.5 2.7 copy.88
  250.2 5.8 %copy.89 = f32[3,8,64,512]{2,3,1,0:T(8,128)} copy(f32[3,8,64,512]{3,2,1,0:T(8,128)} %bitcast.89) | data formatting | bytes 6291456 | tf_op jit(solution)/shard_map/reshape.31
  255.9 4.8 %copy.90 = f32[1,3,512,512]{3,2,1,0:T(8,128)} copy(f32[1,3,512,512]{3,1,2,0:T(4,128)} %bitcast.87) | data formatting | bytes 6291456 | tf_op jit(solution)/shard_map/while
  260.8 5.8 %copy.91 = f32[3,8,64,512]{2,3,1,0:T(8,128)} copy(f32[3,8,64,512]{3,2,1,0:T(8,128)} %bitcast.90) | data formatting | bytes 6291456 | tf_op jit(solution)/shard_map/reshape.26
  266.5 4.9 %copy.92 = f32[1,3,512,512]{3,2,1,0:T(8,128)} copy(f32[1,3,512,512]{3,1,2,0:T(4,128)} %bitcast.93) | data formatting | bytes 6291456 | tf_op jit(solution)/shard_map/while
  271.4 5.8 %copy.93 = f32[3,8,64,512]{2,3,1,0:T(8,128)} copy(f32[3,8,64,512]{3,2,1,0:T(8,128)} %bitcast.91) | data formatting | bytes 6291456 | tf_op jit(solution)/shard_map/reshape.23
  277.2 4.8 %copy.95 = f32[1,3,512,512]{3,2,1,0:T(8,128)} copy(f32[1,3,512,512]{3,1,2,0:T(4,128)} %bitcast.94) | data formatting | bytes 6291456 | tf_op jit(solution)/shard_map/while
  282.0 5.8 %copy.96 = f32[3,8,64,512]{2,3,1,0:T(8,128)} copy(f32[3,8,64,512]{3,2,1,0:T(8,128)} %bitcast.92) | data formatting | bytes 6291456 | tf_op jit(solution)/shard_map/reshape.20
  287.8 10.7 %select_convert_fusion.3 = (bf16[3,8,64,512]{2,3,1,0:T(8,128)(2,1)S(1)}, bf16[3,8,64,512]{2,3,1,0:T(8,128)(2,1)S(1)}) fusion(f32[3,8,64,512]{2,3,1,0:T(8,128)} %copy.89, f32[3,8,64,512]{2,3,1,0:T(8,128)} %copy.91, pred[8,64,512]{1,2,0:T(8,128)(4,1)S(1)} %add_compare_fusion.2, f32[3,8,64,512]{2,3,1,0:T(8,128)} %copy.93, f32[8,64,512]{1,2,0:T(8,128)S(1)} %copy.94, ...), kind=kLoop, calls=%fused_computation.22.clone.1 | loop fusion | flops 12582912 | bytes 18087936 | tf_op jit(solution)/shard_map/convert.4
  298.5 3.6 fusion.85
  302.1 4.1 fusion.86
  307.8 3.9 multiply_reduce_fusion.2
  312.6 1.6 select_reduce_fusion.2
  316.3 16.6 %fusion.84 = (f32[262144]{0:T(1024)}, f32[262144]{0:T(1024)S(1)}, f32[1,1,262144]{2,1,0:T(1,128)}) fusion(bf16[2,2,262144]{2,1,0:T(2,128)(2,1)} %get-tuple-element.387, s32[]{:T(128)} %get-tuple-element.363, s32[]{:T(128)S(6)} %add.959), kind=kLoop, calls=%fused_computation.62.clone.1 | loop fusion | flops 1310720 | bytes 4194312 | tf_op jit(solution)/shard_map/while/body/eval_jaxpr/convert_element_type | solution.py:81
  333.8 1.4 reshape.324
  335.2 1.9 copy.97
  338.7 42.2 %fusion.83 = (f32[3,262144]{1,0:T(4,128)S(1)}, f32[3,262144]{1,0:T(4,128)}) fusion(s32[3]{0:T(128)S(1)} %get-tuple-element.393, s32[262144]{0:T(1024)} %get-tuple-element.394, s32[3]{0:T(128)S(1)} %get-tuple-element.391, s32[262144]{0:T(1024)} %get-tuple-element.392), kind=kLoop, calls=%fused_computation.43.clone.1 | loop fusion | flops 29884416 | bytes 8388632 | tf_op jit(solution)/shard_map/sin | solution.py:37
  380.9 2.7 copy.88
  383.6 5.8 %copy.89 = f32[3,8,64,512]{2,3,1,0:T(8,128)} copy(f32[3,8,64,512]{3,2,1,0:T(8,128)} %bitcast.89) | data formatting | bytes 6291456 | tf_op jit(solution)/shard_map/reshape.31
  389.4 4.8 %copy.90 = f32[1,3,512,512]{3,2,1,0:T(8,128)} copy(f32[1,3,512,512]{3,1,2,0:T(4,128)} %bitcast.87) | data formatting | bytes 6291456 | tf_op jit(solution)/shard_map/while
  394.2 5.8 %copy.91 = f32[3,8,64,512]{2,3,1,0:T(8,128)} copy(f32[3,8,64,512]{3,2,1,0:T(8,128)} %bitcast.90) | data formatting | bytes 6291456 | tf_op jit(solution)/shard_map/reshape.26
  400.0 4.9 %copy.92 = f32[1,3,512,512]{3,2,1,0:T(8,128)} copy(f32[1,3,512,512]{3,1,2,0:T(4,128)} %bitcast.93) | data formatting | bytes 6291456 | tf_op jit(solution)/shard_map/while
  404.9 5.8 %copy.93 = f32[3,8,64,512]{2,3,1,0:T(8,128)} copy(f32[3,8,64,512]{3,2,1,0:T(8,128)} %bitcast.91) | data formatting | bytes 6291456 | tf_op jit(solution)/shard_map/reshape.23
  410.6 4.8 %copy.95 = f32[1,3,512,512]{3,2,1,0:T(8,128)} copy(f32[1,3,512,512]{3,1,2,0:T(4,128)} %bitcast.94) | data formatting | bytes 6291456 | tf_op jit(solution)/shard_map/while
  415.5 5.8 %copy.96 = f32[3,8,64,512]{2,3,1,0:T(8,128)} copy(f32[3,8,64,512]{3,2,1,0:T(8,128)} %bitcast.92) | data formatting | bytes 6291456 | tf_op jit(solution)/shard_map/reshape.20
  421.2 10.7 %select_convert_fusion.3 = (bf16[3,8,64,512]{2,3,1,0:T(8,128)(2,1)S(1)}, bf16[3,8,64,512]{2,3,1,0:T(8,128)(2,1)S(1)}) fusion(f32[3,8,64,512]{2,3,1,0:T(8,128)} %copy.89, f32[3,8,64,512]{2,3,1,0:T(8,128)} %copy.91, pred[8,64,512]{1,2,0:T(8,128)(4,1)S(1)} %add_compare_fusion.2, f32[3,8,64,512]{2,3,1,0:T(8,128)} %copy.93, f32[8,64,512]{1,2,0:T(8,128)S(1)} %copy.94, ...), kind=kLoop, calls=%fused_computation.22.clone.1 | loop fusion | flops 12582912 | bytes 18087936 | tf_op jit(solution)/shard_map/convert.4
  432.0 3.6 fusion.85
  435.6 4.1 fusion.86
  441.3 3.9 multiply_reduce_fusion.2
  446.1 1.6 select_reduce_fusion.2
  (62 shorter events, 14.0 us)
Async XLA Ops:
  7.2 12.7 %copy-start = (bf16[32,2,16384]{2,1,0:T(2,128)(2,1)S(1)}, bf16[32,2,16384]{2,1,0:T(2,128)(2,1)}, u32[]{:S(2)}) copy-start(bf16[32,2,16384]{2,1,0:T(2,128)(2,1)} %param.9) | copy-start | bytes 6291460
  7.2 165.2 %all-reduce.2.cloned.1.call-start = ((), (), s32[]{:S(2)}) async-start(), calls=%async_computation.1 | async-start | bytes 8388608 | tf_op jit(solution)/shard_map/psum | solution.py:18
  18.3 0.7 copy-start.7
  26.0 9.4 %copy-start.2 = (s32[32]{0:T(128)S(1)}, s32[32]{0:T(128)}, u32[]{:S(2)}) copy-start(s32[32]{0:T(128)} %param.10) | copy-start | bytes 388
  26.0 151.3 %all-to-all-start = ((bf16[16,2,2,16384]{3,2,1,0:T(2,128)(2,1)}), bf16[16,2,2,16384]{3,2,1,0:T(2,128)(2,1)}, u32[]{:S(2)}, u32[]{:S(2)}) async-start(bf16[16,2,2,16384]{3,2,1,0:T(2,128)(2,1)} %bitcast.96), calls=%async_computation | async-start | bytes 4194304 | tf_op jit(solution)/shard_map/all_to_all | solution.py:54
  55.6 1.6 copy-start.6
  287.8 10.7 %copy-start.5 = (bf16[8,1024,128]{2,1,0:T(8,128)(2,1)S(1)}, bf16[8,1024,128]{2,1,0:T(8,128)(2,1)}, u32[]{:S(2)}) copy-start(bf16[8,1024,128]{2,1,0:T(8,128)(2,1)} %get-tuple-element.389) | copy-start | bytes 6291460 | tf_op jit(solution)/shard_map/while
  306.2 1.6 copy-start.4
  307.8 4.8 %copy-start.3 = (f32[1,1,262144]{2,1,0:T(1,128)S(1)}, f32[1,1,262144]{2,1,0:T(1,128)}, u32[]{:S(2)}) copy-start(f32[1,1,262144]{2,1,0:T(1,128)} %get-tuple-element.343) | copy-start | bytes 3145732 | tf_op jit(solution)/shard_map/while
  421.2 10.7 %copy-start.5 = (bf16[8,1024,128]{2,1,0:T(8,128)(2,1)S(1)}, bf16[8,1024,128]{2,1,0:T(8,128)(2,1)}, u32[]{:S(2)}) copy-start(bf16[8,1024,128]{2,1,0:T(8,128)(2,1)} %get-tuple-element.389) | copy-start | bytes 6291460 | tf_op jit(solution)/shard_map/while
  439.7 1.6 copy-start.4
  441.3 4.8 %copy-start.3 = (f32[1,1,262144]{2,1,0:T(1,128)S(1)}, f32[1,1,262144]{2,1,0:T(1,128)}, u32[]{:S(2)}) copy-start(f32[1,1,262144]{2,1,0:T(1,128)} %get-tuple-element.343) | copy-start | bytes 3145732 | tf_op jit(solution)/shard_map/while
  449.8 0.5 copy-start.8
  449.8 0.5 copy-start.9
  449.8 1.6 copy-start.1
Sparse Core Ops, SparseCore 0:
  18.5 153.8 all-reduce.1
where the time goes:
time: 464 us; the launch traced here: 458 us
  other arithmetic  195 us (42%)
  waiting for transfers between devices  115 us (25%)
  local copies, waits for them, and re-layouts  106 us (23%)
  matrix products  15.1 us (3%)
  between operations  15.1 us (3%)
  starting transfers between devices  7.82 us (2%)
    psum x1, waiting for transfers between devices, spread(): return lax.psum(block, axis)  115 us
    sin x2, other arithmetic, slide_phases(): return (jnp.cos(angles), jnp.sin(angles))  84.5 us
    another operation x8, local copies, waits for them, and re-layouts  46.1 us
    another operation x9, other arithmetic  40.9 us
    while x20, local copies, waits for them, and re-layouts  35.1 us
    convert_element_type x2, other arithmetic, filter_one(): wave_re = waveform[0].astype(jnp.float32)  33.1 us
    select_n x1, other arithmetic, spread(): jnp.where(lax.axis_index(axis) == owner, block, jnp.zeros_like(block))  10.3 us
  transfers between devices with their start and end apart: 2, of which 1 were waited for; matrix products, arithmetic and copies ran while one was open for 8% of the time, Pallas kernels for 0%

commit v1 on v0

v1 whole, which is shorter than its diff:
```python
import functools

import jax
import jax.numpy as jnp
import numpy as np
from jax import lax
from jax.experimental import pallas as pl
from jax.experimental.pallas import tpu as pltpu
from jax.sharding import PartitionSpec as P

ROWS = 512
COLS = 512
RADIX = 4
FOLD = ROWS // RADIX
WIDE = RADIX * COLS
HALF = COLS // 2

two_pi = 6.283185307179586
eps_norm = 1e-06


def turn_table(left_ids, right_ids, period):
    product_idx = left_ids[:, None] * right_ids[None, :] % period
    angles = product_idx.astype(np.float32) * np.float32(two_pi / period)
    return np.cos(angles), np.sin(angles)


def constant_tables():
    ids = np.arange(ROWS, dtype=np.int32)
    cos, sin = turn_table(ids[:FOLD], ids, ROWS)
    first = []
    for r in range(RADIX):
        c, s = cos[:, r::RADIX], sin[:, r::RADIX]
        first.append(np.concatenate([np.concatenate([c, -s], 1), np.concatenate([s, c], 1)], 0))
    twiddle = np.stack(turn_table(ids, ids, ROWS * COLS))
    cos, sin = turn_table(ids, ids[: HALF + 1], COLS)
    sin = sin[:, :HALF].copy()
    sin[:, 0] = cos[:, HALF]
    second = np.concatenate([cos[:, :HALF], sin], 1)
    return np.stack(first).astype(jnp.bfloat16), twiddle, second.astype(jnp.bfloat16)


def filter_kernel(
    cutoffs, strain, wave, row_phase, col_phase, first, twiddle, second,
    peaks, norms, turned, masked, twisted, total_q, total_r,
):
    dets = strain.shape[0]
    templates = wave.shape[0]
    bins = ROWS * COLS

    def turn(i, _):
        d, rows = i // 8, pl.ds(pl.multiple_of(i % 8 * 16, 16), 16)
        for c in range(WIDE // 512):
            cols = pl.ds(c * 512, 512)
            rr = jnp.concatenate([row_phase[d, 0, rows, :]] * 4, 1)
            ri = jnp.concatenate([row_phase[d, 1, rows, :]] * 4, 1)
            cr, ci = col_phase[d, 0, :, cols], col_phase[d, 1, :, cols]
            pr, pi = rr * cr - ri * ci, rr * ci + ri * cr
            xr = strain[d, 0, rows, cols].astype(jnp.float32)
            xi = strain[d, 1, rows, cols].astype(jnp.float32)
            turned[d, 0, rows, cols] = xr * pr - xi * pi
            turned[d, 1, rows, cols] = xr * pi + xi * pr
        return 0

    lax.fori_loop(0, dets * 8, turn, 0)

    def one_template(t, _):
        cutoff = cutoffs[t]

        def mask(i, acc):
            rows = pl.ds(pl.multiple_of(i * 16, 16), 16)
            for c in range(WIDE // 512):
                cols = pl.ds(c * 512, 512)
                at = (
                    lax.broadcasted_iota(jnp.int32, (16, 512), 0) + i * 16
                ) * WIDE + lax.broadcasted_iota(jnp.int32, (16, 512), 1) + c * 512
                inside = at < cutoff
                wr = jnp.where(inside, wave[t, 0, rows, cols].astype(jnp.float32), 0.0)
                wi = jnp.where(inside, wave[t, 1, rows, cols].astype(jnp.float32), 0.0)
                masked[0, rows, cols] = wr
                masked[1, rows, cols] = wi
                acc = acc + (wr * wr + wi * wi)
            return acc

        acc = lax.fori_loop(0, FOLD // 16, mask, jnp.zeros((16, 512), jnp.float32))
        sigmasq = jnp.sum(acc)

        def one_detector(d, _):
            for c in range(COLS // 256):
                parts = []
                for r in range(RADIX):
                    cols = pl.ds(r * COLS + c * 256, 256)
                    xr, xi = turned[d, 0, :, cols], turned[d, 1, :, cols]
                    wr, wi = masked[0, :, cols], masked[1, :, cols]
                    product = jnp.concatenate([xr * wr + xi * wi, xi * wr - xr * wi], 0)
                    out = jnp.dot(
                        first[r], product.astype(jnp.bfloat16), preferred_element_type=jnp.float32
                    )
                    parts.append((out[:FOLD], out[FOLD:]))
                (r0, i0), (r1, i1), (r2, i2), (r3, i3) = parts
                ar, ai, br, bi = r0 + r2, i0 + i2, r0 - r2, i0 - i2
                cr, ci, dr, di = r1 + r3, i1 + i3, i3 - i1, r1 - r3
                sections = (
                    (ar + cr, ai + ci), (br + dr, bi + di), (ar - cr, ai - ci), (br - dr, bi - di)
                )
                cols = pl.ds(c * 256, 256)
                for q, (sr, si) in enumerate(sections):
                    rows = pl.ds(q * FOLD, FOLD)
                    tc, ts = twiddle[0, rows, cols], twiddle[1, rows, cols]
                    twisted[0, rows, cols] = (sr * tc - si * ts).astype(jnp.bfloat16)
                    twisted[1, rows, cols] = (sr * ts + si * tc).astype(jnp.bfloat16)
            for q in range(RADIX):
                rows = pl.ds(q * FOLD, FOLD)
                ac = jnp.dot(twisted[0, rows, :], second[...], preferred_element_type=jnp.float32)
                db = jnp.dot(twisted[1, rows, :], second[...], preferred_element_type=jnp.float32)
                a, c, dd, b = ac[:, :HALF], ac[:, HALF:], db[:, :HALF], db[:, HALF:]
                ad, bc = a * a + dd * dd, b * b + c * c
                both = ad + bc
                cross = 2.0 * (c * dd - a * b)
                lane = lax.broadcasted_iota(jnp.int32, both.shape, 1)
                edge = lane == 0
                both, cross = jnp.where(edge, 0.5 * both, both), jnp.where(edge, 0.5 * (ad - bc), cross)

                @pl.when(d == 0)
                def _():
                    total_q[rows, :] = both
                    total_r[rows, :] = cross

                @pl.when(d > 0)
                def _():
                    total_q[rows, :] += both
                    total_r[rows, :] += cross
            return 0

        lax.fori_loop(0, dets, one_detector, 0)

        def largest(i, acc):
            rows = pl.ds(pl.multiple_of(i * 32, 32), 32)
            return jnp.maximum(acc, total_q[rows, :] + jnp.abs(total_r[rows, :]))

        best = lax.fori_loop(0, ROWS // 32, largest, jnp.zeros((32, HALF), jnp.float32))
        peaks[t] = jnp.max(best) / (2.0 * (sigmasq + eps_norm))
        norms[t] = sigmasq / bins
        return 0

    lax.fori_loop(0, templates, one_template, 0)


def run_filter(cutoffs, strain, wave, row_phase, col_phase):
    templates, dets = wave.shape[0], strain.shape[0]
    first, twiddle, second = constant_tables()
    vmem = pl.BlockSpec(memory_space=pltpu.VMEM)
    smem = pl.BlockSpec(memory_space=pltpu.SMEM)
    out = jax.ShapeDtypeStruct((templates,), jnp.float32)
    return pl.pallas_call(
        filter_kernel,
        out_shape=(out, out),
        in_specs=[smem] + [vmem] * 7,
        out_specs=(smem, smem),
        scratch_shapes=[
            pltpu.VMEM((dets, 2, FOLD, WIDE), jnp.float32),
            pltpu.VMEM((2, FOLD, WIDE), jnp.float32),
            pltpu.VMEM((2, ROWS, COLS), jnp.bfloat16),
            pltpu.VMEM((ROWS, HALF), jnp.float32),
            pltpu.VMEM((ROWS, HALF), jnp.float32),
        ],
        compiler_params=pltpu.CompilerParams(vmem_limit_bytes=56 * 1024 * 1024),
        name="filter",
    )(cutoffs, strain, wave, row_phase, col_phase, jnp.asarray(first), jnp.asarray(twiddle), jnp.asarray(second))


def phases(slides):
    total = ROWS * COLS
    slides = slides[:, None]
    row = jnp.arange(FOLD, dtype=jnp.int32)[None] * slides % FOLD
    col = jnp.arange(WIDE, dtype=jnp.int32)[None] * slides % total
    row = row.astype(jnp.float32) * (two_pi / FOLD)
    col = col.astype(jnp.float32) * (two_pi / total)
    row = jnp.stack([jnp.cos(row), jnp.sin(row)], 1)
    col = jnp.stack([jnp.cos(col), jnp.sin(col)], 1)
    return jnp.broadcast_to(row[..., None], row.shape + (128,)), col[:, :, None, :]


def body(strain_slots, templates, cutoffs, lists, owner, slides):
    devices = lax.axis_size("tpl")
    own_index = lax.axis_index("tpl")
    per_device = lists.shape[1]
    chosen = lists.reshape(-1)
    dets = strain_slots.shape[1]
    strain = strain_slots[0].reshape(dets, 2, FOLD, WIDE)
    strain = jnp.where(own_index == owner[0], strain, jnp.zeros_like(strain))
    strain = lax.psum(strain, "tpl")
    rows = templates.shape[2] // WIDE
    picked = templates[chosen].reshape(devices, per_device, 2, rows, WIDE)
    arrived = lax.all_to_all(picked, "tpl", split_axis=0, concat_axis=3, tiled=True)[0]
    own_ids = lax.dynamic_index_in_dim(lists, own_index, 0, keepdims=False)
    row_phase, col_phase = phases(slides)
    return run_filter(cutoffs[own_ids], strain, arrived, row_phase, col_phase)


def solution(mesh):
    in_specs = (
        P(("grp", "tpl"), None, None, None),
        P(None, None, "tpl"),
        P(),
        P(),
        P("grp"),
        P("grp"),
    )
    out_specs = (P(("grp", "tpl")), P(("grp", "tpl")))
    return jax.shard_map(body, mesh=mesh, in_specs=in_specs, out_specs=out_specs, check_vma=False)
```

time: 464 us -> 196 us (0.42); the launches traced: 458 us -> 196 us
  other arithmetic: 195 us -> 5.21 us
  local copies, waits for them, and re-layouts: 106 us -> 24.9 us
  Pallas kernels: 0 us -> 21.2 us
  matrix products: 15.1 us -> 0 us
  waiting for transfers between devices: 115 us -> 122 us
    sin x4 -> x0, other arithmetic: 92.7 us -> none  [the longest x2 84.5 us: slide_phases(): return (jnp.cos(angles), jnp.sin(angles))]
    another operation x8 -> x0, local copies, waits for them, and re-layouts: 46.1 us -> none
    another operation x9 -> x2, other arithmetic: 40.9 us -> 0.06 us  [the longest x1 0.05 us: phases(): col = jnp.stack([jnp.cos(col), jnp.sin(col)], 1)]
    convert_element_type x3 -> x0, other arithmetic: 38.1 us -> none  [the longest x2 33.1 us: filter_one(): wave_re = waveform[0].astype(jnp.float32)]
    all_to_all x1, waiting for transfers between devices: 0.01 us -> 36.6 us  [body(): lax.all_to_all(picked, 'tpl', split_axis=0, concat_axis=3, tiled=True)[0]]
    while x20 -> x0, local copies, waits for them, and re-layouts: 35.1 us -> none
    psum x1, waiting for transfers between devices: 115 us -> 85.5 us  [body(): strain = lax.psum(strain, 'tpl')]
    pallas_call x0 -> x1, Pallas kernels: none -> 21.2 us  [run_filter(): pl.pallas_call(filter_kernel, out_shape=(out, out), in_specs=[smem] + [vm...]
  transfers between devices with their start and end apart: 2 -> 2, of which waited for: 1 -> 2; matrix products, arithmetic and copies ran while one was open for 8% -> 8% of each run, Pallas kernels for 0% -> 0%
where the time goes in v1:
time: 196 us
  waiting for transfers between devices  122 us (62%)
  local copies, waits for them, and re-layouts  24.9 us (13%)
  Pallas kernels  21.2 us (11%)
  between operations  14.8 us (8%)
  starting transfers between devices  7.51 us (4%)
  other arithmetic  5.21 us (3%)
    psum x1, waiting for transfers between devices, body(): strain = lax.psum(strain, 'tpl')  85.5 us
    all_to_all x1, waiting for transfers between devices, body(): lax.all_to_all(picked, 'tpl', split_axis=0, concat_axis=3, tiled=True)[0]  36.6 us
    pallas_call x1, Pallas kernels, run_filter(): pl.pallas_call(filter_kernel, out_shape=(out, out), in_specs=[smem] + [vm...  21.2 us
    all_to_all x1, starting transfers between devices, body(): lax.all_to_all(picked, 'tpl', split_axis=0, concat_axis=3, tiled=True)[0]  7.46 us
    gather x1, local copies, waits for them, and re-layouts, body(): picked = templates[chosen].reshape(devices, per_device, 2, rows, WIDE)  6.2 us
    select_n x1, local copies, waits for them, and re-layouts, body(): strain = jnp.where(own_index == owner[0], strain, jnp.zeros_like(strain))  5.88 us
    reshape x1, local copies, waits for them, and re-layouts, body(): picked = templates[chosen].reshape(devices, per_device, 2, rows, WIDE)  4.49 us
    select_n x1, other arithmetic, body(): strain = jnp.where(own_index == owner[0], strain, jnp.zeros_like(strain))  4.15 us
  transfers between devices with their start and end apart: 2, of which 2 were waited for; matrix products, arithmetic and copies ran while one was open for 8% of the time, Pallas kernels for 0%

profile of v1, /device:TPU:0, one launch (start us, length us, event | category | flops | bytes accessed | tf_op | source)
XLA Modules:
  0.0 195.7 jit_solution(5108237303952891615)
XLA Ops:
  7.2 0.0 copy-start
  7.2 0.9 copy.15
  8.1 0.1 reshape.251
  8.2 0.6 copy-done
  8.8 6.2 %gather_fusion.1 = bf16[32,2,16384]{2,1,0:T(2,128)(2,1)} fusion(bf16[32,2,16384]{2,1,0:T(2,128)(2,1)S(1)} %copy-done, s32[1024]{0:T(1024)S(1)} %pad_clamp_fusion), kind=kCustom, calls=%fused_computation.1 | custom fusion | bytes 4194432 | tf_op jit(solution)/shard_map/gather | solution.py:194
  15.0 4.5 %reshape.252 = bf16[16,2,2,8,2048]{4,3,2,1,0:T(8,128)(2,1)} reshape(bf16[32,2,16384]{2,1,0:T(2,128)(2,1)} %gather_fusion.1) | data formatting | bytes 4194304 | tf_op jit(solution)/shard_map/reshape | solution.py:194
  19.5 7.5 %all-to-all-start = ((bf16[16,2,2,8,2048]{4,3,2,1,0:T(8,128)(2,1)}), bf16[16,2,2,8,2048]{4,3,2,1,0:T(8,128)(2,1)}, u32[]{:S(2)}, u32[]{:S(2)}) async-start(bf16[16,2,2,8,2048]{4,3,2,1,0:T(8,128)(2,1)} %reshape.252), calls=%async_computation | async-start | bytes 4194304 | tf_op jit(solution)/shard_map/all_to_all | solution.py:195
  26.9 0.0 all-reduce.2.cloned.1.call-start
  27.6 4.1 %broadcast_select_fusion = bf16[1,3,2,262144]{3,2,1,0:T(2,128)(2,1)} fusion(bf16[1,3,2,262144]{3,2,1,0:T(2,128)(2,1)} %param.9, pred[]{:T(512)S(6)} %eq.7), kind=kLoop, calls=%fused_computation.2 | loop fusion | flops 1572864 | bytes 6291457 | tf_op jit(solution)/shard_map/jit(_where)/select_n | solution.py:191
  31.8 5.9 %select_n.74 = bf16[3,2,128,2048]{3,2,1,0:T(8,128)(2,1)} reshape(bf16[1,3,2,262144]{3,2,1,0:T(2,128)(2,1)} %broadcast_select_fusion) | data formatting | bytes 6291456 | tf_op jit(solution)/shard_map/jit(_where)/select_n | solution.py:191
  37.7 0.0 copy-start.3
  37.7 0.0 copy-start.2
  37.7 0.0 copy-start.1
  37.7 0.0 all-reduce.2.cloned.1.call-update
  37.7 0.6 copy-done.3
  38.3 0.8 fusion.4
  39.2 0.0 copy-done.2
  39.2 0.2 dynamic-slice_reduce_fusion
  39.4 0.6 broadcast_in_dim.8.col_phase
  40.1 0.0 copy-done.1
  40.1 1.2 gather_fusion
  41.2 0.1 fusion.9
  41.4 36.6 %all-to-all-done = bf16[16,2,2,8,2048]{4,3,2,1,0:T(8,128)(2,1)} async-done(((bf16[16,2,2,8,2048]{4,3,2,1,0:T(8,128)(2,1)}), bf16[16,2,2,8,2048]{4,3,2,1,0:T(8,128)(2,1)}, u32[]{:S(2)}, u32[]{:S(2)}) %all-to-all-start) | async-done | bytes 2097184 | tf_op jit(solution)/shard_map/all_to_all | solution.py:195
  78.0 3.2 %copy_bitcast_fusion.wave = bf16[2,2,128,2048]{3,2,1,0:T(8,128)(2,1)} fusion(bf16[16,2,2,8,2048]{4,3,2,1,0:T(8,128)(2,1)} %all-to-all-done), kind=kLoop, calls=%fused_computation.3 | loop fusion | bytes 4194304 | tf_op jit(solution)/shard_map/squeeze | solution.py:195
  81.2 85.5 %all-reduce.2.cloned.1.call-done.strain = bf16[3,2,128,2048]{3,2,1,0:T(8,128)(2,1)} async-done(((bf16[3,2,128,2048]{3,2,1,0:T(8,128)(2,1)}), bf16[3,2,128,2048]{3,2,1,0:T(8,128)(2,1)}) %all-reduce.2.cloned.1.call-update) | async-done | bytes 3145744 | tf_op jit(solution)/shard_map/psum | solution.py:192
  166.7 0.9 broadcast_in_dim.7.row_phase
  167.6 21.2 %filter.1 = (f32[2]{0:T(128)}, f32[2]{0:T(128)}) custom-call(s32[2]{0:T(128)} %gather_fusion, bf16[3,2,128,2048]{3,2,1,0:T(8,128)(2,1)} %all-reduce.2.cloned.1.call-done.strain, bf16[2,2,128,2048]{3,2,1,0:T(8,128)(2,1)} %copy_bitcast_fusion.wave, f32[3,2,128,128]{3,2,1,0:T(8,128)} %broadcast_in_dim.7.row_phase, f32[3,2,1,2048]{3,2,1,0:T(1,128)} %broadcast_in_dim.8.col_phase, ...), custom_call_target="tpu_custom_call" | custom-call | tf_op jit(solution)/shard_map/filter/pallas_call | solution.py:155
  (6 shorter events, 0.1 us)
Async XLA Ops:
  7.2 1.6 copy-start
  19.5 58.5 %all-to-all-start = ((bf16[16,2,2,8,2048]{4,3,2,1,0:T(8,128)(2,1)}), bf16[16,2,2,8,2048]{4,3,2,1,0:T(8,128)(2,1)}, u32[]{:S(2)}, u32[]{:S(2)}) async-start(bf16[16,2,2,8,2048]{4,3,2,1,0:T(8,128)(2,1)} %reshape.252), calls=%async_computation | async-start | bytes 4194304 | tf_op jit(solution)/shard_map/all_to_all | solution.py:195
  26.9 139.7 %all-reduce.2.cloned.1.call-start = ((), (), s32[]{:S(2)}) async-start(), calls=%async_computation.1 | async-start | bytes 6291456 | tf_op jit(solution)/shard_map/psum | solution.py:192
  37.7 0.7 copy-start.3
  37.7 1.5 copy-start.2
  37.7 2.4 %copy-start.1 = (s32[32]{0:T(128)S(1)}, s32[32]{0:T(128)}, u32[]{:S(2)}) copy-start(s32[32]{0:T(128)} %param.11) | copy-start | bytes 388
Sparse Core Ops, SparseCore 0:
  37.8 128.8 all-reduce.1

commit v2 on v1

--- a/solution.py
+++ b/solution.py
@@ -67,22 +67,28 @@
     def one_template(t, _):
         cutoff = cutoffs[t]
 
+        blocks = 8 // wave.shape[3]
+
         def mask(i, acc):
-            rows = pl.ds(pl.multiple_of(i * 16, 16), 16)
+            rows = pl.ds(pl.multiple_of(i * 8, 8), 8)
             for c in range(WIDE // 512):
                 cols = pl.ds(c * 512, 512)
                 at = (
-                    lax.broadcasted_iota(jnp.int32, (16, 512), 0) + i * 16
-                ) * WIDE + lax.broadcasted_iota(jnp.int32, (16, 512), 1) + c * 512
+                    lax.broadcasted_iota(jnp.int32, (8, 512), 0) + i * 8
+                ) * WIDE + lax.broadcasted_iota(jnp.int32, (8, 512), 1) + c * 512
                 inside = at < cutoff
-                wr = jnp.where(inside, wave[t, 0, rows, cols].astype(jnp.float32), 0.0)
-                wi = jnp.where(inside, wave[t, 1, rows, cols].astype(jnp.float32), 0.0)
-                masked[0, rows, cols] = wr
-                masked[1, rows, cols] = wi
-                acc = acc + (wr * wr + wi * wi)
+                parts = []
+                for p in range(2):
+                    got = [
+                        wave[t, p, i * blocks + e, :, cols].astype(jnp.float32) for e in range(blocks)
+                    ]
+                    got = got[0] if blocks == 1 else jnp.concatenate(got, 0)
+                    parts.append(jnp.where(inside, got, 0.0))
+                    masked[p, rows, cols] = parts[p]
+                acc = acc + (parts[0] * parts[0] + parts[1] * parts[1])
             return acc
 
-        acc = lax.fori_loop(0, FOLD // 16, mask, jnp.zeros((16, 512), jnp.float32))
+        acc = lax.fori_loop(0, FOLD // 8, mask, jnp.zeros((8, 512), jnp.float32))
         sigmasq = jnp.sum(acc)
 
         def one_detector(d, _):
@@ -181,18 +187,289 @@
     return jnp.broadcast_to(row[..., None], row.shape + (128,)), col[:, :, None, :]
 
 
-def body(strain_slots, templates, cutoffs, lists, owner, slides):
+MESH = pl.DeviceIdType.MESH
+
+
+def share_kernel(
+    width_y, flags, strain, picked, full, arrived, other, ring_in, first_out,
+    core_send, core_recv, sum_send, sum_recv, all_send, all_recv, part_send, part_recv,
+    swap_send, swap_recv, own_sem, cross_send, cross_recv,
+):
+    n, groups = lax.axis_size("tpl"), lax.axis_size("grp")
+    me, group = lax.axis_index("tpl"), lax.axis_index("grp")
+    chips = n // 2
+    core, chip = me % 2, me // 2
+    depth = chips // width_y
+    y, z = chip % width_y, chip // width_y
+    pos = z + y * (2 * depth - 1 - 2 * z)
+    half = strain.shape[1] // 2
+    prow, pcol = ring_in.shape[3], ring_in.shape[4]
+    colparts = strain.shape[2] // pcol
+    subs = strain.shape[0] // 2
+    share = arrived.shape[0] // groups
+    mine = pl.ds(group * share, share)
+    partner = me + 1 - 2 * core
+
+    def device_at(p):
+        p = (p + chips) % chips
+        yy = p // depth
+        zz = p + yy * (2 * depth - 1 - 2 * p)
+        return (zz * width_y + yy) * 2 + core
+
+    nexts = (device_at(pos + 1), device_at(pos - 1))
+
+    def chunk(direction, back):
+        return (pos - back + 2 * chips) % chips if direction == 0 else (pos + back) % chips
+
+    def spot(base, j):
+        rows = pl.multiple_of(base + j // colparts * prow, prow)
+        return pl.ds(rows, prow), pl.ds(pl.multiple_of(j % colparts * pcol, pcol), pcol)
+
+    def piece(ref, base, direction, k, j):
+        return ref.at[(direction * subs + k,) + spot(base, j)]
+
+    def remote(src, dst, send, recv, **where):
+        return pltpu.make_async_remote_copy(
+            src_ref=src, dst_ref=dst, send_sem=send, recv_sem=recv,
+            device_id=where, device_id_type=MESH,
+        )
+
+    def core_copy(direction, back):
+        j = chunk(direction, back)
+        planes = pl.ds(direction * subs, subs)
+        return remote(
+            strain.at[(planes,) + spot((1 - core) * half, j)],
+            other.at[(planes,) + spot(0, j)],
+            core_send.at[back, direction], core_recv.at[back, direction], tpl=partner,
+        )
+
+    def sum_copy(direction, k, s):
+        src = first_out.at[direction, k]
+        if not isinstance(s, int):
+            src = ring_in.at[s - 1, direction, k]
+        return remote(
+            src, ring_in.at[s, direction, k],
+            sum_send.at[s, direction, k], sum_recv.at[s, direction, k], tpl=nexts[direction],
+        )
+
+    def all_copy(direction, k, s):
+        at = piece(full, core * half, direction, k, chunk(direction, s))
+        return remote(
+            at, at, all_send.at[s, direction, k], all_recv.at[s, direction, k], tpl=nexts[direction]
+        )
+
+    def part_copy(direction, k, s, base):
+        at = piece(full, base, direction, k, chunk(direction, s))
+        return remote(
+            at, at, part_send.at[s, direction, k], part_recv.at[s, direction, k], tpl=partner
+        )
+
+    def swap_copy(i):
+        to = (me - i + n) % n
+        return remote(
+            picked.at[to, mine], arrived.at[mine, me], swap_send.at[i], swap_recv.at[i], tpl=to
+        )
+
+    def swap_arrival(i):
+        source = (me + i) % n
+        return remote(
+            picked.at[me, mine], arrived.at[mine, source], swap_send.at[i], swap_recv.at[i], tpl=source
+        )
+
+    def cross_copy(i, g):
+        at = arrived.at[mine, (me + i) % n]
+        return remote(
+            at, at, cross_send.at[g - 1, i], cross_recv.at[g - 1, i], grp=(group + g) % groups
+        )
+
+    def cross_arrival(i, g):
+        source = (group - g + groups) % groups
+        at = arrived.at[pl.ds(source * share, share), (me + i) % n]
+        return remote(at, at, cross_send.at[g - 1, i], cross_recv.at[g - 1, i], grp=source)
+
+    barrier = pltpu.get_barrier_semaphore()
+
+    def greet(i, _):
+        pl.semaphore_signal(barrier, inc=1, device_id={"tpl": (me + i) % n}, device_id_type=MESH)
+        return 0
+
+    lax.fori_loop(1, n, greet, 0)
+    for g in range(1, groups):
+        pl.semaphore_signal(
+            barrier, inc=1, device_id={"grp": (group + g) % groups}, device_id_type=MESH
+        )
+    pl.semaphore_wait(barrier, n - 1 + groups - 1)
+
+    own = pltpu.make_async_copy(picked.at[me], arrived.at[:, me], own_sem)
+    own.start()
+
+    def start_core(i, _):
+        for direction in range(2):
+            core_copy(direction, i + 1 - (i + 1) // chips * chips).start()
+        return 0
+
+    lax.fori_loop(0, chips, start_core, 0)
+    i_own, chip_owns = flags[0], flags[1]
+
+    def candidate(direction, k, j):
+        here = piece(strain, core * half, direction, k, j)[...]
+        there = piece(other, 0, direction, k, j)[...]
+        return jnp.where(i_own != 0, here, there)
+
+    for direction in range(2):
+        core_copy(direction, 1).wait_recv()
+        for k in range(subs):
+            first_out[direction, k] = candidate(direction, k, chunk(direction, 1))
+            sum_copy(direction, k, 0).start()
+
+    def start_swap(i, _):
+        swap_copy(i).start()
+        return 0
+
+    lax.fori_loop(1, n, start_swap, 0)
+
+    def joined(direction, k, s, j):
+        remote(
+            first_out.at[direction, k], ring_in.at[s, direction, k],
+            sum_send.at[s, direction, k], sum_recv.at[s, direction, k], tpl=nexts[direction],
+        ).wait_recv()
+        return jnp.where(chip_owns != 0, candidate(direction, k, j), ring_in[s, direction, k])
+
+    def sum_step(s, _):
+        for direction in range(2):
+            core_copy(direction, s + 2).wait_recv()
+        for k in range(subs):
+            for direction in range(2):
+                ring_in[s, direction, k] = joined(direction, k, s, chunk(direction, s + 2))
+                sum_copy(direction, k, s + 1).start()
+        return 0
+
+    lax.fori_loop(0, chips - 2, sum_step, 0)
+    for direction in range(2):
+        core_copy(direction, 0).wait_recv()
+    for k in range(subs):
+        for direction in range(2):
+            piece(full, core * half, direction, k, pos)[...] = joined(direction, k, chips - 2, pos)
+            all_copy(direction, k, 0).start()
+            part_copy(direction, k, 0, core * half).start()
+
+    def cross_start(i):
+        swap_arrival(i).wait_recv()
+        for g in range(1, groups):
+            cross_copy(i, g).start()
+
+    per_step = (n - 1) // (chips - 1)
+
+    def all_step(s, _):
+        for k in range(subs):
+            for direction in range(2):
+                at = piece(full, core * half, direction, k, chunk(direction, s + 1))
+                remote(
+                    at, at, all_send.at[s, direction, k], all_recv.at[s, direction, k],
+                    tpl=nexts[direction],
+                ).wait_recv()
+                all_copy(direction, k, s + 1).start()
+                part_copy(direction, k, s + 1, core * half).start()
+        for e in range(per_step):
+            cross_start(1 + s * per_step + e)
+        return 0
+
+    lax.fori_loop(0, chips - 2, all_step, 0)
+    last = chips - 2
+    for k in range(subs):
+        for direction in range(2):
+            at = piece(full, core * half, direction, k, chunk(direction, last + 1))
+            remote(
+                at, at, all_send.at[last, direction, k], all_recv.at[last, direction, k],
+                tpl=nexts[direction],
+            ).wait_recv()
+            part_copy(direction, k, last + 1, core * half).start()
+    for i in range(1 + last * per_step, n):
+        cross_start(i)
+
+    def finish(s, _):
+        for direction in range(2):
+            core_copy(direction, s).wait_send()
+            for k in range(subs):
+                part_copy(direction, k, s, core * half).wait_send()
+                part_copy(direction, k, s, (1 - core) * half).wait_recv()
+        return 0
+
+    lax.fori_loop(0, chips, finish, 0)
+
+    def finish_ring(s, _):
+        for direction in range(2):
+            for k in range(subs):
+                all_copy(direction, k, s).wait_send()
+                remote(
+                    first_out.at[direction, k], ring_in.at[s, direction, k],
+                    sum_send.at[s, direction, k], sum_recv.at[s, direction, k], tpl=nexts[direction],
+                ).wait_send()
+        return 0
+
+    lax.fori_loop(0, chips - 1, finish_ring, 0)
+
+    def finish_swap(i, _):
+        swap_copy(i).wait_send()
+        for g in range(1, groups):
+            cross_copy(i, g).wait_send()
+            cross_arrival(i, g).wait_recv()
+        return 0
+
+    lax.fori_loop(1, n, finish_swap, 0)
+    own.wait()
+
+
+def run_share(width_y, flags, strain, picked):
+    n, groups = lax.axis_size("tpl"), lax.axis_size("grp")
+    chips = n // 2
+    planes, high, wide = strain.shape
+    subs = planes // 2
+    rowparts = max(1, chips * 256 // wide)
+    prow, pcol = high // 2 // rowparts, wide * rowparts // chips
+    vmem = pl.BlockSpec(memory_space=pltpu.VMEM)
+    dma = pltpu.SemaphoreType.DMA
+    arrived = (picked.shape[1], n) + picked.shape[2:]
+    return pl.pallas_call(
+        functools.partial(share_kernel, width_y),
+        out_shape=(
+            jax.ShapeDtypeStruct(strain.shape, strain.dtype),
+            jax.ShapeDtypeStruct(arrived, picked.dtype),
+        ),
+        in_specs=[pl.BlockSpec(memory_space=pltpu.SMEM), vmem, vmem],
+        out_specs=(vmem, vmem),
+        scratch_shapes=[
+            pltpu.VMEM((planes, high // 2, wide), strain.dtype),
+            pltpu.VMEM((chips - 1, 2, subs, prow, pcol), strain.dtype),
+            pltpu.VMEM((2, subs, prow, pcol), strain.dtype),
+            dma((chips, 2)), dma((chips, 2)),
+            dma((chips - 1, 2, subs)), dma((chips - 1, 2, subs)),
+            dma((chips - 1, 2, subs)), dma((chips - 1, 2, subs)),
+            dma((chips, 2, subs)), dma((chips, 2, subs)),
+            dma((n,)), dma((n,)), dma,
+            dma((max(1, groups - 1), n)), dma((max(1, groups - 1), n)),
+        ],
+        compiler_params=pltpu.CompilerParams(
+            collective_id=0, has_side_effects=True, vmem_limit_bytes=40 * 1024 * 1024
+        ),
+        name="share",
+    )(flags, strain, picked)
+
+
+def body(width_y, strain_slots, templates, cutoffs, lists, owner, slides):
     devices = lax.axis_size("tpl")
     own_index = lax.axis_index("tpl")
     per_device = lists.shape[1]
     chosen = lists.reshape(-1)
     dets = strain_slots.shape[1]
-    strain = strain_slots[0].reshape(dets, 2, FOLD, WIDE)
-    strain = jnp.where(own_index == owner[0], strain, jnp.zeros_like(strain))
-    strain = lax.psum(strain, "tpl")
+    strain = strain_slots[0].reshape(dets * 2, FOLD, WIDE)
+    flags = jnp.stack([own_index == owner[0], own_index // 2 == owner[0] // 2]).astype(jnp.int32)
     rows = templates.shape[2] // WIDE
-    picked = templates[chosen].reshape(devices, per_device, 2, rows, WIDE)
-    arrived = lax.all_to_all(picked, "tpl", split_axis=0, concat_axis=3, tiled=True)[0]
+    picked = templates.reshape(-1, 2, rows, WIDE)[chosen]
+    picked = picked.reshape(devices, per_device * 2, rows, WIDE)
+    strain, arrived = run_share(width_y, flags, strain, picked)
+    strain = strain.reshape(dets, 2, FOLD, WIDE)
+    arrived = arrived.reshape(per_device, 2, devices, rows, WIDE)
     own_ids = lax.dynamic_index_in_dim(lists, own_index, 0, keepdims=False)
     row_phase, col_phase = phases(slides)
     return run_filter(cutoffs[own_ids], strain, arrived, row_phase, col_phase)
@@ -208,4 +485,5 @@
         P("grp"),
     )
     out_specs = (P(("grp", "tpl")), P(("grp", "tpl")))
-    return jax.shard_map(body, mesh=mesh, in_specs=in_specs, out_specs=out_specs, check_vma=False)
+    width_y = len({d.coords[1] for d in mesh.devices[0].flat})
+    return jax.shard_map(functools.partial(body, width_y), mesh=mesh, in_specs=in_specs, out_specs=out_specs, check_vma=False)

time: 196 us -> 128 us (0.65)
  waiting for transfers between devices: 122 us -> 0 us
  Pallas kernels: 21.2 us -> 105 us
  between operations: 14.8 us -> 1.4 us
  starting transfers between devices: 7.51 us -> 0 us
  other arithmetic: 5.21 us -> 1.14 us
  local copies, waits for them, and re-layouts: 24.9 us -> 21 us
    psum x1 -> x0, waiting for transfers between devices: 85.5 us -> none  [body(): strain = lax.psum(strain, 'tpl')]
    pallas_call x0 -> x1, Pallas kernels: none -> 81.9 us  [run_share(): pl.pallas_call(functools.partial(share_kernel, width_y), out_shape=(jax.S...]
    all_to_all x1 -> x0, waiting for transfers between devices: 36.6 us -> none  [body(): lax.all_to_all(picked, 'tpl', split_axis=0, concat_axis=3, tiled=True)[0]]
    all_to_all x1 -> x0, starting transfers between devices: 7.46 us -> none  [body(): lax.all_to_all(picked, 'tpl', split_axis=0, concat_axis=3, tiled=True)[0]]
    select_n x1 -> x0, local copies, waits for them, and re-layouts: 5.88 us -> none  [body(): strain = jnp.where(own_index == owner[0], strain, jnp.zeros_like(strain))]
    another operation x0 -> x1, local copies, waits for them, and re-layouts: none -> 4.5 us  [body(): strain = strain_slots[0].reshape(dets * 2, FOLD, WIDE)]
    select_n x2 -> x1, other arithmetic: 4.15 us -> 0.01 us  [body(): picked = templates.reshape(-1, 2, rows, WIDE)[chosen]]
    squeeze x1 -> x0, local copies, waits for them, and re-layouts: 3.21 us -> none  [body(): lax.all_to_all(picked, 'tpl', split_axis=0, concat_axis=3, tiled=True)[0]]
  transfers between devices with their start and end apart: 2 -> 0, of which waited for: 2 -> 0; matrix products, arithmetic and copies ran while one was open for 8% -> 0% of each run, Pallas kernels for 0% -> 0%
where the time goes in v2:
time: 128 us
  Pallas kernels  105 us (82%)
  local copies, waits for them, and re-layouts  21 us (16%)
  between operations  1.4 us (1%)
    pallas_call x1, Pallas kernels, run_share(): pl.pallas_call(functools.partial(share_kernel, width_y), out_shape=(jax.S...  81.9 us
    pallas_call x1, Pallas kernels, run_filter(): pl.pallas_call(filter_kernel, out_shape=(out, out), in_specs=[smem] + [vm...  22.6 us
    unnamed x13, local copies, waits for them, and re-layouts  4.67 us
    another operation x1, local copies, waits for them, and re-layouts, body(): strain = strain_slots[0].reshape(dets * 2, FOLD, WIDE)  4.5 us
    reshape x1, local copies, waits for them, and re-layouts, body(): picked = templates.reshape(-1, 2, rows, WIDE)[chosen]  4.48 us
    gather x1, local copies, waits for them, and re-layouts, body(): picked = templates.reshape(-1, 2, rows, WIDE)[chosen]  3.58 us

profile of v2, /device:TPU:0, one launch (start us, length us, event | category | flops | bytes accessed | tf_op | source)
XLA Modules:
  0.0 128.0 jit_solution(7196307384497934334)
XLA Ops:
  0.6 0.0 copy-start
  0.6 0.9 dynamic-slice_reduce_fusion
  1.5 0.0 copy-done
  1.5 1.2 gather_fusion
  3.4 0.1 add_convert_fusion.flags
  3.5 4.5 %reshape_squeeze.3.strain = bf16[6,128,2048]{2,1,0:T(8,128)(2,1)S(1)} reshape(bf16[1,3,2,262144]{3,2,1,0:T(2,128)(2,1)} %param.9) | data formatting | bytes 6291456 | tf_op jit(solution)/shard_map/reshape;squeeze | solution.py:465
  8.0 0.0 copy-start.4
  8.0 4.5 %reshape.256 = bf16[32,2,8,2048]{3,2,1,0:T(8,128)(2,1)} reshape(bf16[32,2,16384]{2,1,0:T(2,128)(2,1)} %param.10) | data formatting | bytes 4194304 | tf_op jit(solution)/shard_map/reshape | solution.py:468
  12.5 0.0 copy-done.4
  12.5 0.1 copy.12
  12.6 0.1 reshape.257
  12.7 3.6 %gather_fusion.1 = bf16[32,2,8,2048]{3,2,1,0:T(8,128)(2,1)} fusion(bf16[32,2,8,2048]{3,2,1,0:T(8,128)(2,1)} %reshape.256, s32[1024]{0:T(1024)S(1)} %pad_clamp_fusion), kind=kCustom, calls=%fused_computation.1 | custom fusion | bytes 4194432 | tf_op jit(solution)/shard_map/gather | solution.py:468
  16.3 0.0 copy-start.1
  16.3 1.6 %copy-done.1 = bf16[32,2,8,2048]{3,2,1,0:T(8,128)(2,1)S(1)} copy-done((bf16[32,2,8,2048]{3,2,1,0:T(8,128)(2,1)S(1)}, bf16[32,2,8,2048]{3,2,1,0:T(8,128)(2,1)}, u32[]{:S(2)}) %copy-start.1) | copy-done | bytes 2097176
  17.9 0.0 copy-start.5
  17.9 81.9 %share.1 = (bf16[6,128,2048]{2,1,0:T(8,128)(2,1)S(1)}, bf16[4,16,8,2048]{3,2,1,0:T(8,128)(2,1)S(1)}) custom-call(s32[2]{0:T(128)S(1)} %add_convert_fusion.flags, bf16[6,128,2048]{2,1,0:T(8,128)(2,1)S(1)} %reshape_squeeze.3.strain, bf16[16,4,8,2048]{3,2,1,0:T(8,128)(2,1)S(1)} %bitcast.17), custom_call_target="tpu_custom_call" | custom-call | tf_op jit(solution)/shard_map/share/pallas_call | solution.py:433
  99.8 0.0 copy-start.2
  99.8 1.6 %copy-done.2 = bf16[6,128,2048]{2,1,0:T(8,128)(2,1)} copy-done((bf16[6,128,2048]{2,1,0:T(8,128)(2,1)}, bf16[6,128,2048]{2,1,0:T(8,128)(2,1)S(1)}, u32[]{:S(2)}) %copy-start.2) | copy-done | bytes 3145752
  101.5 0.0 copy-start.3
  101.5 1.3 %copy-done.3 = bf16[4,16,8,2048]{3,2,1,0:T(8,128)(2,1)} copy-done((bf16[4,16,8,2048]{3,2,1,0:T(8,128)(2,1)}, bf16[4,16,8,2048]{3,2,1,0:T(8,128)(2,1)S(1)}, u32[]{:S(2)}) %copy-start.3) | copy-done | bytes 2097176
  102.8 0.0 copy-done.5
  102.8 0.1 fusion.9
  102.9 0.9 broadcast_in_dim.4.row_phase
  103.9 0.8 fusion.4
  104.7 0.1 pad_maximum_fusion
  104.8 0.6 broadcast_in_dim.5.col_phase
  105.4 22.6 %filter.1 = (f32[2]{0:T(128)}, f32[2]{0:T(128)}) custom-call(s32[2]{0:T(128)} %gather_fusion, bf16[3,2,128,2048]{3,2,1,0:T(8,128)(2,1)} %bitcast.18, bf16[2,2,16,8,2048]{4,3,2,1,0:T(8,128)(2,1)} %bitcast.19, f32[3,2,128,128]{3,2,1,0:T(8,128)} %broadcast_in_dim.4.row_phase, f32[3,2,1,2048]{3,2,1,0:T(1,128)} %broadcast_in_dim.5.col_phase, ...), custom_call_target="tpu_custom_call" | custom-call | tf_op jit(solution)/shard_map/filter/pallas_call | solution.py:161
  (5 shorter events, 0.0 us)
Async XLA Ops:
  0.6 0.9 copy-start
  8.0 4.5 %copy-start.4 = (s32[16,2]{0,1:T(2,128)S(1)}, s32[16,2]{0,1:T(2,128)}, u32[]{:S(2)}) copy-start(s32[16,2]{0,1:T(2,128)} %param.12) | copy-start | bytes 388
  16.3 1.6 %copy-start.1 = (bf16[32,2,8,2048]{3,2,1,0:T(8,128)(2,1)S(1)}, bf16[32,2,8,2048]{3,2,1,0:T(8,128)(2,1)}, u32[]{:S(2)}) copy-start(bf16[32,2,8,2048]{3,2,1,0:T(8,128)(2,1)} %gather_fusion.1) | copy-start | bytes 6291460
  17.9 84.9 %copy-start.5 = (s32[3]{0:T(128)S(1)}, s32[3]{0:T(128)}, u32[]{:S(2)}) copy-start(s32[3]{0:T(128)} %param.14) | copy-start | bytes 40
  99.8 1.7 %copy-start.2 = (bf16[6,128,2048]{2,1,0:T(8,128)(2,1)}, bf16[6,128,2048]{2,1,0:T(8,128)(2,1)S(1)}, u32[]{:S(2)}) copy-start(bf16[6,128,2048]{2,1,0:T(8,128)(2,1)S(1)} %get-tuple-element.4) | copy-start | bytes 9437188
  101.5 1.3 %copy-start.3 = (bf16[4,16,8,2048]{3,2,1,0:T(8,128)(2,1)}, bf16[4,16,8,2048]{3,2,1,0:T(8,128)(2,1)S(1)}, u32[]{:S(2)}) copy-start(bf16[4,16,8,2048]{3,2,1,0:T(8,128)(2,1)S(1)} %get-tuple-element.5) | copy-start | bytes 6291460

commit v3 on v2

--- a/solution.py
+++ b/solution.py
@@ -170,7 +170,7 @@
             pltpu.VMEM((ROWS, HALF), jnp.float32),
             pltpu.VMEM((ROWS, HALF), jnp.float32),
         ],
-        compiler_params=pltpu.CompilerParams(vmem_limit_bytes=56 * 1024 * 1024),
+        compiler_params=pltpu.CompilerParams(vmem_limit_bytes=30 * 1024 * 1024),
         name="filter",
     )(cutoffs, strain, wave, row_phase, col_phase, jnp.asarray(first), jnp.asarray(twiddle), jnp.asarray(second))
 
@@ -191,7 +191,7 @@
 
 
 def share_kernel(
-    width_y, flags, strain, picked, full, arrived, other, ring_in, first_out,
+    width_y, flags, chosen, strain, bank, full, arrived, picked, other, ring_in, first_out,
     core_send, core_recv, sum_send, sum_recv, all_send, all_recv, part_send, part_recv,
     swap_send, swap_recv, own_sem, cross_send, cross_recv,
 ):
@@ -300,9 +300,6 @@
         )
     pl.semaphore_wait(barrier, n - 1 + groups - 1)
 
-    own = pltpu.make_async_copy(picked.at[me], arrived.at[:, me], own_sem)
-    own.start()
-
     def start_core(i, _):
         for direction in range(2):
             core_copy(direction, i + 1 - (i + 1) // chips * chips).start()
@@ -310,6 +307,37 @@
 
     lax.fori_loop(0, chips, start_core, 0)
     i_own, chip_owns = flags[0], flags[1]
+    slots = picked.shape[1] // 2
+
+    def gather(i, _):
+        for e in range(slots):
+            picked[i, pl.ds(2 * e, 2)] = bank[chosen[i * slots + e]]
+        return 0
+
+    lax.fori_loop(0, n, gather, 0)
+    own = pltpu.make_async_copy(picked.at[me], arrived.at[:, me], own_sem)
+    own.start()
+    per_step = -(-(n - 1) // (chips - 3))
+
+    def cross_start(i):
+        swap_arrival(i).wait_recv()
+        for g in range(1, groups):
+            cross_copy(i, g).start()
+
+    def templates_on(step):
+        for e in range(per_step):
+            at = 1 + step * per_step + e
+
+            @pl.when(at < n)
+            def _():
+                swap_copy(at).start()
+
+        for e in range(2):
+            late = 1 + (step - 3) * 2 + e
+
+            @pl.when((late >= 1) & (late < n))
+            def _():
+                cross_start(late)
 
     def candidate(direction, k, j):
         here = piece(strain, core * half, direction, k, j)[...]
@@ -321,12 +349,6 @@
         for k in range(subs):
             first_out[direction, k] = candidate(direction, k, chunk(direction, 1))
             sum_copy(direction, k, 0).start()
-
-    def start_swap(i, _):
-        swap_copy(i).start()
-        return 0
-
-    lax.fori_loop(1, n, start_swap, 0)
 
     def joined(direction, k, s, j):
         remote(
@@ -342,6 +364,7 @@
             for direction in range(2):
                 ring_in[s, direction, k] = joined(direction, k, s, chunk(direction, s + 2))
                 sum_copy(direction, k, s + 1).start()
+        templates_on(s)
         return 0
 
     lax.fori_loop(0, chips - 2, sum_step, 0)
@@ -352,13 +375,6 @@
             piece(full, core * half, direction, k, pos)[...] = joined(direction, k, chips - 2, pos)
             all_copy(direction, k, 0).start()
             part_copy(direction, k, 0, core * half).start()
-
-    def cross_start(i):
-        swap_arrival(i).wait_recv()
-        for g in range(1, groups):
-            cross_copy(i, g).start()
-
-    per_step = (n - 1) // (chips - 1)
 
     def all_step(s, _):
         for k in range(subs):
@@ -370,8 +386,7 @@
                 ).wait_recv()
                 all_copy(direction, k, s + 1).start()
                 part_copy(direction, k, s + 1, core * half).start()
-        for e in range(per_step):
-            cross_start(1 + s * per_step + e)
+        templates_on(chips - 2 + s)
         return 0
 
     lax.fori_loop(0, chips - 2, all_step, 0)
@@ -384,8 +399,6 @@
                 tpl=nexts[direction],
             ).wait_recv()
             part_copy(direction, k, last + 1, core * half).start()
-    for i in range(1 + last * per_step, n):
-        cross_start(i)
 
     def finish(s, _):
         for direction in range(2):
@@ -420,7 +433,7 @@
     own.wait()
 
 
-def run_share(width_y, flags, strain, picked):
+def run_share(width_y, flags, chosen, strain, bank):
     n, groups = lax.axis_size("tpl"), lax.axis_size("grp")
     chips = n // 2
     planes, high, wide = strain.shape
@@ -429,16 +442,18 @@
     prow, pcol = high // 2 // rowparts, wide * rowparts // chips
     vmem = pl.BlockSpec(memory_space=pltpu.VMEM)
     dma = pltpu.SemaphoreType.DMA
-    arrived = (picked.shape[1], n) + picked.shape[2:]
+    pieces = chosen.shape[0] // n * 2
+    arrived = (pieces, n) + bank.shape[2:]
     return pl.pallas_call(
         functools.partial(share_kernel, width_y),
         out_shape=(
             jax.ShapeDtypeStruct(strain.shape, strain.dtype),
-            jax.ShapeDtypeStruct(arrived, picked.dtype),
+            jax.ShapeDtypeStruct(arrived, bank.dtype),
         ),
-        in_specs=[pl.BlockSpec(memory_space=pltpu.SMEM), vmem, vmem],
+        in_specs=[pl.BlockSpec(memory_space=pltpu.SMEM)] * 2 + [vmem, vmem],
         out_specs=(vmem, vmem),
         scratch_shapes=[
+            pltpu.VMEM((n, pieces) + bank.shape[2:], bank.dtype),
             pltpu.VMEM((planes, high // 2, wide), strain.dtype),
             pltpu.VMEM((chips - 1, 2, subs, prow, pcol), strain.dtype),
             pltpu.VMEM((2, subs, prow, pcol), strain.dtype),
@@ -450,10 +465,10 @@
             dma((max(1, groups - 1), n)), dma((max(1, groups - 1), n)),
         ],
         compiler_params=pltpu.CompilerParams(
-            collective_id=0, has_side_effects=True, vmem_limit_bytes=40 * 1024 * 1024
+            collective_id=0, has_side_effects=True, vmem_limit_bytes=22 * 1024 * 1024
         ),
         name="share",
-    )(flags, strain, picked)
+    )(flags, chosen, strain, bank)
 
 
 def body(width_y, strain_slots, templates, cutoffs, lists, owner, slides):
@@ -465,9 +480,8 @@
     strain = strain_slots[0].reshape(dets * 2, FOLD, WIDE)
     flags = jnp.stack([own_index == owner[0], own_index // 2 == owner[0] // 2]).astype(jnp.int32)
     rows = templates.shape[2] // WIDE
-    picked = templates.reshape(-1, 2, rows, WIDE)[chosen]
-    picked = picked.reshape(devices, per_device * 2, rows, WIDE)
-    strain, arrived = run_share(width_y, flags, strain, picked)
+    bank = templates.reshape(-1, 2, rows, WIDE)
+    strain, arrived = run_share(width_y, flags, chosen, strain, bank)
     strain = strain.reshape(dets, 2, FOLD, WIDE)
     arrived = arrived.reshape(per_device, 2, devices, rows, WIDE)
     own_ids = lax.dynamic_index_in_dim(lists, own_index, 0, keepdims=False)

time: 128 us -> 112 us (0.88)
  Pallas kernels: 105 us -> 95.9 us
  local copies, waits for them, and re-layouts: 21 us -> 13.1 us
    pallas_call x1, Pallas kernels: 81.9 us -> 75.5 us  [run_share(): pl.pallas_call(functools.partial(share_kernel, width_y), out_shape=(jax.S...]
    gather x1 -> x0, local copies, waits for them, and re-layouts: 3.58 us -> none  [body(): picked = templates.reshape(-1, 2, rows, WIDE)[chosen]]
    unnamed x13, local copies, waits for them, and re-layouts: 4.67 us -> 2.37 us
    pallas_call x1, Pallas kernels: 22.6 us -> 20.4 us  [run_filter(): pl.pallas_call(filter_kernel, out_shape=(out, out), in_specs=[smem] + [vm...]
where the time goes in v3:
time: 112 us
  Pallas kernels  95.9 us (86%)
  local copies, waits for them, and re-layouts  13.1 us (12%)
  between operations  1.43 us (1%)
  other arithmetic  1.13 us (1%)
    pallas_call x1, Pallas kernels, run_share(): pl.pallas_call(functools.partial(share_kernel, width_y), out_shape=(jax.S...  75.5 us
    pallas_call x1, Pallas kernels, run_filter(): pl.pallas_call(filter_kernel, out_shape=(out, out), in_specs=[smem] + [vm...  20.4 us
    another operation x1, local copies, waits for them, and re-layouts, body(): strain = strain_slots[0].reshape(dets * 2, FOLD, WIDE)  4.51 us
    reshape x1, local copies, waits for them, and re-layouts, body(): bank = templates.reshape(-1, 2, rows, WIDE)  4.47 us
    unnamed x13, local copies, waits for them, and re-layouts  2.37 us

profile of v3, /device:TPU:0, one launch (start us, length us, event | category | flops | bytes accessed | tf_op | source)
XLA Modules:
  0.0 111.6 jit_solution(6671289352600293974)
XLA Ops:
  0.6 0.0 copy-start
  0.6 0.9 dynamic-slice_reduce_fusion
  1.5 0.0 copy-done
  1.5 0.6 gather_fusion
  2.9 0.1 add_convert_fusion.flags
  2.9 0.8 copy.12
  3.7 0.1 reshape.225.chosen
  3.8 4.5 %reshape_squeeze.3.strain = bf16[6,128,2048]{2,1,0:T(8,128)(2,1)S(1)} reshape(bf16[1,3,2,262144]{3,2,1,0:T(2,128)(2,1)} %param.9) | data formatting | bytes 6291456 | tf_op jit(solution)/shard_map/reshape;squeeze | solution.py:480
  8.3 4.5 %reshape.226.bank = bf16[32,2,8,2048]{3,2,1,0:T(8,128)(2,1)} reshape(bf16[32,2,16384]{2,1,0:T(2,128)(2,1)} %param.10) | data formatting | bytes 4194304 | tf_op jit(solution)/shard_map/reshape | solution.py:483
  12.8 0.0 copy-start.1
  12.8 1.6 %copy-done.1 = bf16[32,2,8,2048]{3,2,1,0:T(8,128)(2,1)S(1)} copy-done((bf16[32,2,8,2048]{3,2,1,0:T(8,128)(2,1)S(1)}, bf16[32,2,8,2048]{3,2,1,0:T(8,128)(2,1)}, u32[]{:S(2)}) %copy-start.1) | copy-done | bytes 2097176
  14.4 0.0 copy-start.5
  14.4 0.0 copy-start.2
  14.4 0.0 copy-start.3
  14.4 0.0 copy-start.4
  14.4 75.5 %share.1 = (bf16[6,128,2048]{2,1,0:T(8,128)(2,1)S(1)}, bf16[4,16,8,2048]{3,2,1,0:T(8,128)(2,1)S(1)}) custom-call(s32[2]{0:T(128)S(1)} %add_convert_fusion.flags, s32[32]{0:T(128)S(1)} %reshape.225.chosen, bf16[6,128,2048]{2,1,0:T(8,128)(2,1)S(1)} %reshape_squeeze.3.strain, bf16[32,2,8,2048]{3,2,1,0:T(8,128)(2,1)S(1)} %copy-done.1), custom_call_target="tpu_custom_call" | custom-call | tf_op jit(solution)/shard_map/share/pallas_call | solution.py:447
  89.9 0.0 copy-done.5
  89.9 0.1 fusion.9
  90.1 0.2 broadcast_in_dim.4.row_phase
  90.2 0.8 fusion.4
  91.1 0.1 pad_maximum_fusion
  91.2 0.0 copy-done.2
  91.2 0.0 copy-done.3
  91.2 0.0 copy-done.4
  91.2 20.4 %filter.1 = (f32[2]{0:T(128)}, f32[2]{0:T(128)}) custom-call(s32[2]{0:T(128)S(1)} %gather_fusion, bf16[3,2,128,2048]{3,2,1,0:T(8,128)(2,1)S(1)} %bitcast.14, bf16[2,2,16,8,2048]{4,3,2,1,0:T(8,128)(2,1)S(1)} %bitcast.15, f32[3,2,128,128]{3,2,1,0:T(8,128)S(1)} %broadcast_in_dim.4.row_phase, f32[3,2,1,2048]{3,2,1,0:T(1,128)S(1)} %broadcast_in_dim.5.col_phase, ...), custom_call_target="tpu_custom_call" | custom-call | tf_op jit(solution)/shard_map/filter/pallas_call | solution.py:161
  (4 shorter events, 0.1 us)
Async XLA Ops:
  0.6 0.9 copy-start
  12.8 1.6 %copy-start.1 = (bf16[32,2,8,2048]{3,2,1,0:T(8,128)(2,1)S(1)}, bf16[32,2,8,2048]{3,2,1,0:T(8,128)(2,1)}, u32[]{:S(2)}) copy-start(bf16[32,2,8,2048]{3,2,1,0:T(8,128)(2,1)} %reshape.226.bank) | copy-start | bytes 6291460
  14.4 75.6 %copy-start.5 = (s32[3]{0:T(128)S(1)}, s32[3]{0:T(128)}, u32[]{:S(2)}) copy-start(s32[3]{0:T(128)} %param.14) | copy-start | bytes 40
  14.4 76.8 %copy-start.2 = (f32[2,512,512]{2,1,0:T(8,128)S(1)}, f32[2,512,512]{2,1,0:T(8,128)}, u32[]{:S(2)}) copy-start(f32[2,512,512]{2,1,0:T(8,128)} %constant.72.clone.twiddle) | copy-start | bytes 6291460
  14.4 76.8 %copy-start.3 = (bf16[4,256,256]{2,1,0:T(8,128)(2,1)S(1)}, bf16[4,256,256]{2,1,0:T(8,128)(2,1)}, u32[]{:S(2)}) copy-start(bf16[4,256,256]{2,1,0:T(8,128)(2,1)} %constant.71.clone.first) | copy-start | bytes 1572868
  14.4 76.9 %copy-start.4 = (bf16[512,512]{1,0:T(8,128)(2,1)S(1)}, bf16[512,512]{1,0:T(8,128)(2,1)}, u32[]{:S(2)}) copy-start(bf16[512,512]{1,0:T(8,128)(2,1)} %constant.73.clone.second) | copy-start | bytes 1572868

commit v4 on v3

--- a/solution.py
+++ b/solution.py
@@ -205,7 +205,8 @@
     half = strain.shape[1] // 2
     prow, pcol = ring_in.shape[3], ring_in.shape[4]
     colparts = strain.shape[2] // pcol
-    subs = strain.shape[0] // 2
+    subs = strain.shape[0]
+    arm = chips // 2
     share = arrived.shape[0] // groups
     mine = pl.ds(group * share, share)
     partner = me + 1 - 2 * core
@@ -226,7 +227,7 @@
         return pl.ds(rows, prow), pl.ds(pl.multiple_of(j % colparts * pcol, pcol), pcol)
 
     def piece(ref, base, direction, k, j):
-        return ref.at[(direction * subs + k,) + spot(base, j)]
+        return ref.at[(k,) + spot(base, j)]
 
     def remote(src, dst, send, recv, **where):
         return pltpu.make_async_remote_copy(
@@ -234,19 +235,20 @@
             device_id=where, device_id_type=MESH,
         )
 
-    def core_copy(direction, back):
-        j = chunk(direction, back)
-        planes = pl.ds(direction * subs, subs)
+    def core_copy(back):
+        j = chunk(0, back)
+        planes = pl.ds(0, subs)
         return remote(
             strain.at[(planes,) + spot((1 - core) * half, j)],
             other.at[(planes,) + spot(0, j)],
-            core_send.at[back, direction], core_recv.at[back, direction], tpl=partner,
-        )
-
-    def sum_copy(direction, k, s):
-        src = first_out.at[direction, k]
-        if not isinstance(s, int):
-            src = ring_in.at[s - 1, direction, k]
+            core_send.at[back], core_recv.at[back], tpl=partner,
+        )
+
+    def covered(direction, k):
+        return (k < subs // 2) == (direction == 0)
+
+    def sum_copy(direction, k, s, started=False):
+        src = first_out.at[direction, k] if started else ring_in.at[max(s - 1, 0), direction, k]
         return remote(
             src, ring_in.at[s, direction, k],
             sum_send.at[s, direction, k], sum_recv.at[s, direction, k], tpl=nexts[direction],
@@ -300,13 +302,13 @@
         )
     pl.semaphore_wait(barrier, n - 1 + groups - 1)
 
-    def start_core(i, _):
-        for direction in range(2):
-            core_copy(direction, i + 1 - (i + 1) // chips * chips).start()
-        return 0
-
-    lax.fori_loop(0, chips, start_core, 0)
-    i_own, chip_owns = flags[0], flags[1]
+    order = [arm]
+    for h in range(arm - 1, 0, -1):
+        order += [h, chips - h]
+    order.append(0)
+    for back in order:
+        core_copy(back).start()
+    i_own, chip_owns, from_left = flags[0], flags[1], flags[2]
     slots = picked.shape[1] // 2
 
     def gather(i, _):
@@ -317,7 +319,8 @@
     lax.fori_loop(0, n, gather, 0)
     own = pltpu.make_async_copy(picked.at[me], arrived.at[:, me], own_sem)
     own.start()
-    per_step = -(-(n - 1) // (chips - 3))
+    per_step = -(-(n - 1) // (arm - 1))
+    late_step = -(-(n - 1) // (2 * arm - 3))
 
     def cross_start(i):
         swap_arrival(i).wait_recv()
@@ -325,102 +328,81 @@
             cross_copy(i, g).start()
 
     def templates_on(step):
-        for e in range(per_step):
-            at = 1 + step * per_step + e
-
-            @pl.when(at < n)
-            def _():
-                swap_copy(at).start()
-
-        for e in range(2):
-            late = 1 + (step - 3) * 2 + e
-
-            @pl.when((late >= 1) & (late < n))
-            def _():
-                cross_start(late)
+        for at in range(1 + step * per_step, min(n, 1 + (step + 1) * per_step)):
+            swap_copy(at).start()
+        late = 1 + (step - 2) * late_step
+        for at in range(max(late, 1), min(n, late + late_step)):
+            cross_start(at)
 
     def candidate(direction, k, j):
         here = piece(strain, core * half, direction, k, j)[...]
         there = piece(other, 0, direction, k, j)[...]
         return jnp.where(i_own != 0, here, there)
 
-    for direction in range(2):
-        core_copy(direction, 1).wait_recv()
-        for k in range(subs):
-            first_out[direction, k] = candidate(direction, k, chunk(direction, 1))
-            sum_copy(direction, k, 0).start()
-
-    def joined(direction, k, s, j):
-        remote(
-            first_out.at[direction, k], ring_in.at[s, direction, k],
-            sum_send.at[s, direction, k], sum_recv.at[s, direction, k], tpl=nexts[direction],
-        ).wait_recv()
-        return jnp.where(chip_owns != 0, candidate(direction, k, j), ring_in[s, direction, k])
-
-    def sum_step(s, _):
-        for direction in range(2):
-            core_copy(direction, s + 2).wait_recv()
+    core_copy(arm).wait_recv()
+    for k in range(subs):
+        direction = 0 if covered(0, k) else 1
+        first_out[direction, k] = candidate(direction, k, chunk(1, arm))
+        sum_copy(direction, k, 0, True).start()
+    for back in (arm - 1, chips - arm + 1):
+        core_copy(back).wait_recv()
+    for k in range(subs):
+        direction = 1 if covered(0, k) else 0
+        first_out[direction, k] = candidate(direction, k, chunk(1 - direction, arm - 1))
+        sum_copy(direction, k, 1, True).start()
+    for s in range(arm - 1):
+        h = arm - 1 - s
+        if s > 0:
+            for back in (h, chips - h):
+                core_copy(back).wait_recv()
         for k in range(subs):
             for direction in range(2):
-                ring_in[s, direction, k] = joined(direction, k, s, chunk(direction, s + 2))
-                sum_copy(direction, k, s + 1).start()
+                if s > 0 or covered(direction, k):
+                    sum_copy(direction, k, s).wait_recv()
+                    ring_in[s, direction, k] = jnp.where(
+                        chip_owns != 0,
+                        candidate(direction, k, chunk(1 - direction, h)),
+                        ring_in[s, direction, k],
+                    )
+                    sum_copy(direction, k, s + 1).start()
         templates_on(s)
-        return 0
-
-    lax.fori_loop(0, chips - 2, sum_step, 0)
-    for direction in range(2):
-        core_copy(direction, 0).wait_recv()
+    core_copy(0).wait_recv()
     for k in range(subs):
         for direction in range(2):
-            piece(full, core * half, direction, k, pos)[...] = joined(direction, k, chips - 2, pos)
+            sum_copy(direction, k, arm - 1).wait_recv()
+        left = from_left + (flags[3] if covered(0, k) else 0)
+        best = jnp.where(left != 0, ring_in[arm - 1, 0, k], ring_in[arm - 1, 1, k])
+        piece(full, core * half, 0, k, pos)[...] = jnp.where(
+            chip_owns != 0, candidate(0, k, pos), best
+        )
+        for direction in range(2):
             all_copy(direction, k, 0).start()
-            part_copy(direction, k, 0, core * half).start()
-
-    def all_step(s, _):
+        part_copy(0, k, 0, core * half).start()
+    for s in range(arm):
         for k in range(subs):
             for direction in range(2):
-                at = piece(full, core * half, direction, k, chunk(direction, s + 1))
-                remote(
-                    at, at, all_send.at[s, direction, k], all_recv.at[s, direction, k],
-                    tpl=nexts[direction],
-                ).wait_recv()
-                all_copy(direction, k, s + 1).start()
-                part_copy(direction, k, s + 1, core * half).start()
-        templates_on(chips - 2 + s)
-        return 0
-
-    lax.fori_loop(0, chips - 2, all_step, 0)
-    last = chips - 2
-    for k in range(subs):
-        for direction in range(2):
-            at = piece(full, core * half, direction, k, chunk(direction, last + 1))
-            remote(
-                at, at, all_send.at[last, direction, k], all_recv.at[last, direction, k],
-                tpl=nexts[direction],
-            ).wait_recv()
-            part_copy(direction, k, last + 1, core * half).start()
-
-    def finish(s, _):
-        for direction in range(2):
-            core_copy(direction, s).wait_send()
-            for k in range(subs):
-                part_copy(direction, k, s, core * half).wait_send()
-                part_copy(direction, k, s, (1 - core) * half).wait_recv()
-        return 0
-
-    lax.fori_loop(0, chips, finish, 0)
-
-    def finish_ring(s, _):
-        for direction in range(2):
-            for k in range(subs):
-                all_copy(direction, k, s).wait_send()
-                remote(
-                    first_out.at[direction, k], ring_in.at[s, direction, k],
-                    sum_send.at[s, direction, k], sum_recv.at[s, direction, k], tpl=nexts[direction],
-                ).wait_send()
-        return 0
-
-    lax.fori_loop(0, chips - 1, finish_ring, 0)
+                if s < arm - 1 or covered(direction, k):
+                    at = piece(full, core * half, direction, k, chunk(direction, s + 1))
+                    remote(
+                        at, at, all_send.at[s, direction, k], all_recv.at[s, direction, k],
+                        tpl=nexts[direction],
+                    ).wait_recv()
+                    if s + 1 < arm - 1 or (s + 1 == arm - 1 and covered(direction, k)):
+                        all_copy(direction, k, s + 1).start()
+                    part_copy(direction, k, s + 1, core * half).start()
+        templates_on(arm - 1 + s)
+    for back in range(chips):
+        core_copy(back).wait_send()
+    for s in range(arm + 1):
+        for k in range(subs):
+            for direction in range(2):
+                if (s == 0 and direction == 0) or 0 < s < arm or (s == arm and covered(direction, k)):
+                    part_copy(direction, k, s, core * half).wait_send()
+                    part_copy(direction, k, s, (1 - core) * half).wait_recv()
+                if s < arm - 1 or (s == arm - 1 and covered(direction, k)):
+                    all_copy(direction, k, s).wait_send()
+                if 0 < s < arm or (s == 0 and covered(direction, k)):
+                    sum_copy(direction, k, s).wait_send()
 
     def finish_swap(i, _):
         swap_copy(i).wait_send()
@@ -437,7 +419,7 @@
     n, groups = lax.axis_size("tpl"), lax.axis_size("grp")
     chips = n // 2
     planes, high, wide = strain.shape
-    subs = planes // 2
+    subs = planes
     rowparts = max(1, chips * 256 // wide)
     prow, pcol = high // 2 // rowparts, wide * rowparts // chips
     vmem = pl.BlockSpec(memory_space=pltpu.VMEM)
@@ -455,12 +437,12 @@
         scratch_shapes=[
             pltpu.VMEM((n, pieces) + bank.shape[2:], bank.dtype),
             pltpu.VMEM((planes, high // 2, wide), strain.dtype),
-            pltpu.VMEM((chips - 1, 2, subs, prow, pcol), strain.dtype),
+            pltpu.VMEM((chips // 2, 2, subs, prow, pcol), strain.dtype),
             pltpu.VMEM((2, subs, prow, pcol), strain.dtype),
-            dma((chips, 2)), dma((chips, 2)),
-            dma((chips - 1, 2, subs)), dma((chips - 1, 2, subs)),
-            dma((chips - 1, 2, subs)), dma((chips - 1, 2, subs)),
-            dma((chips, 2, subs)), dma((chips, 2, subs)),
+            dma((chips,)), dma((chips,)),
+            dma((chips // 2, 2, subs)), dma((chips // 2, 2, subs)),
+            dma((chips // 2, 2, subs)), dma((chips // 2, 2, subs)),
+            dma((chips // 2 + 1, 2, subs)), dma((chips // 2 + 1, 2, subs)),
             dma((n,)), dma((n,)), dma,
             dma((max(1, groups - 1), n)), dma((max(1, groups - 1), n)),
         ],
@@ -478,7 +460,16 @@
     chosen = lists.reshape(-1)
     dets = strain_slots.shape[1]
     strain = strain_slots[0].reshape(dets * 2, FOLD, WIDE)
-    flags = jnp.stack([own_index == owner[0], own_index // 2 == owner[0] // 2]).astype(jnp.int32)
+    chips = devices // 2
+    depth = chips // width_y
+
+    def place(device):
+        chip = device // 2
+        return chip // width_y + chip % width_y * (2 * depth - 1 - 2 * (chip // width_y))
+
+    ahead = (place(owner[0]) - place(own_index)) % chips
+    flags = jnp.stack([own_index == owner[0], ahead == 0, ahead > chips // 2, ahead == chips // 2])
+    flags = flags.astype(jnp.int32)
     rows = templates.shape[2] // WIDE
     bank = templates.reshape(-1, 2, rows, WIDE)
     strain, arrived = run_share(width_y, flags, chosen, strain, bank)

time: 112 us -> 108 us (0.964)
  Pallas kernels: 95.9 us -> 91.8 us
    pallas_call x1, Pallas kernels: 75.5 us -> 72.1 us  [run_share(): pl.pallas_call(functools.partial(share_kernel, width_y), out_shape=(jax.S...]
where the time goes in v4:
time: 108 us
  Pallas kernels  91.8 us (85%)
  local copies, waits for them, and re-layouts  13.1 us (12%)
  between operations  1.52 us (1%)
  other arithmetic  1.13 us (1%)
    pallas_call x1, Pallas kernels, run_share(): pl.pallas_call(functools.partial(share_kernel, width_y), out_shape=(jax.S...  72.1 us
    pallas_call x1, Pallas kernels, run_filter(): pl.pallas_call(filter_kernel, out_shape=(out, out), in_specs=[smem] + [vm...  19.7 us
    another operation x1, local copies, waits for them, and re-layouts, body(): strain = strain_slots[0].reshape(dets * 2, FOLD, WIDE)  4.51 us
    reshape x1, local copies, waits for them, and re-layouts, body(): bank = templates.reshape(-1, 2, rows, WIDE)  4.47 us
    unnamed x13, local copies, waits for them, and re-layouts  2.37 us

profile of v4, /device:TPU:0, one launch (start us, length us, event | category | flops | bytes accessed | tf_op | source)
XLA Modules:
  0.0 107.6 jit_solution(14488757607101674445)
XLA Ops:
  0.6 0.0 copy-start
  0.6 0.9 dynamic-slice_reduce_fusion
  1.5 0.0 copy-done
  1.5 0.6 gather_fusion
  2.9 0.1 add_convert_fusion.flags
  3.0 0.8 copy.12
  3.8 0.1 reshape.225.chosen
  3.9 4.5 %reshape_squeeze.3.strain = bf16[6,128,2048]{2,1,0:T(8,128)(2,1)S(1)} reshape(bf16[1,3,2,262144]{3,2,1,0:T(2,128)(2,1)} %param.9) | data formatting | bytes 6291456 | tf_op jit(solution)/shard_map/reshape;squeeze | solution.py:462
  8.4 4.5 %reshape.226.bank = bf16[32,2,8,2048]{3,2,1,0:T(8,128)(2,1)} reshape(bf16[32,2,16384]{2,1,0:T(2,128)(2,1)} %param.10) | data formatting | bytes 4194304 | tf_op jit(solution)/shard_map/reshape | solution.py:474
  12.9 0.0 copy-start.1
  12.9 1.6 %copy-done.1 = bf16[32,2,8,2048]{3,2,1,0:T(8,128)(2,1)S(1)} copy-done((bf16[32,2,8,2048]{3,2,1,0:T(8,128)(2,1)S(1)}, bf16[32,2,8,2048]{3,2,1,0:T(8,128)(2,1)}, u32[]{:S(2)}) %copy-start.1) | copy-done | bytes 2097176
  14.5 0.0 copy-start.5
  14.5 0.0 copy-start.2
  14.5 0.0 copy-start.3
  14.5 0.0 copy-start.4
  14.5 72.1 %share.1 = (bf16[6,128,2048]{2,1,0:T(8,128)(2,1)S(1)}, bf16[4,16,8,2048]{3,2,1,0:T(8,128)(2,1)S(1)}) custom-call(s32[4]{0:T(128)S(1)} %add_convert_fusion.flags, s32[32]{0:T(128)S(1)} %reshape.225.chosen, bf16[6,128,2048]{2,1,0:T(8,128)(2,1)S(1)} %reshape_squeeze.3.strain, bf16[32,2,8,2048]{3,2,1,0:T(8,128)(2,1)S(1)} %copy-done.1), custom_call_target="tpu_custom_call" | custom-call | tf_op jit(solution)/shard_map/share/pallas_call | solution.py:429
  86.6 0.0 copy-done.5
  86.6 0.1 fusion.9
  86.8 0.2 broadcast_in_dim.4.row_phase
  86.9 0.8 fusion.4
  87.8 0.1 pad_maximum_fusion
  87.9 0.0 copy-done.2
  87.9 0.0 copy-done.3
  87.9 0.0 copy-done.4
  87.9 19.7 %filter.1 = (f32[2]{0:T(128)}, f32[2]{0:T(128)}) custom-call(s32[2]{0:T(128)S(1)} %gather_fusion, bf16[3,2,128,2048]{3,2,1,0:T(8,128)(2,1)S(1)} %bitcast.16, bf16[2,2,16,8,2048]{4,3,2,1,0:T(8,128)(2,1)S(1)} %bitcast.17, f32[3,2,128,128]{3,2,1,0:T(8,128)S(1)} %broadcast_in_dim.4.row_phase, f32[3,2,1,2048]{3,2,1,0:T(1,128)S(1)} %broadcast_in_dim.5.col_phase, ...), custom_call_target="tpu_custom_call" | custom-call | tf_op jit(solution)/shard_map/filter/pallas_call | solution.py:161
  (4 shorter events, 0.1 us)
Async XLA Ops:
  0.6 0.9 copy-start
  12.9 1.6 %copy-start.1 = (bf16[32,2,8,2048]{3,2,1,0:T(8,128)(2,1)S(1)}, bf16[32,2,8,2048]{3,2,1,0:T(8,128)(2,1)}, u32[]{:S(2)}) copy-start(bf16[32,2,8,2048]{3,2,1,0:T(8,128)(2,1)} %reshape.226.bank) | copy-start | bytes 6291460
  14.5 72.2 %copy-start.5 = (s32[3]{0:T(128)S(1)}, s32[3]{0:T(128)}, u32[]{:S(2)}) copy-start(s32[3]{0:T(128)} %param.14) | copy-start | bytes 40
  14.5 73.4 %copy-start.2 = (f32[2,512,512]{2,1,0:T(8,128)S(1)}, f32[2,512,512]{2,1,0:T(8,128)}, u32[]{:S(2)}) copy-start(f32[2,512,512]{2,1,0:T(8,128)} %constant.118.clone.twiddle) | copy-start | bytes 6291460
  14.5 73.5 %copy-start.3 = (bf16[4,256,256]{2,1,0:T(8,128)(2,1)S(1)}, bf16[4,256,256]{2,1,0:T(8,128)(2,1)}, u32[]{:S(2)}) copy-start(bf16[4,256,256]{2,1,0:T(8,128)(2,1)} %constant.117.clone.first) | copy-start | bytes 1572868
  14.5 73.5 %copy-start.4 = (bf16[512,512]{1,0:T(8,128)(2,1)S(1)}, bf16[512,512]{1,0:T(8,128)(2,1)}, u32[]{:S(2)}) copy-start(bf16[512,512]{1,0:T(8,128)(2,1)} %constant.119.clone.second) | copy-start | bytes 1572868
